TPU v7x, 32 devices: a whole 2x2x4 slice. The times are simulated.
32 devices in a mesh: dp: 8 (over z, x), tensor: 4 (over y, core).
Axes of the slice: x: 2, y: 2, z: 4, core: 2. Of those that a mesh axis runs over, the one named last changes fastest.
Arguments:
- tokens: bfloat16 [8192, 1024], P(('dp', 'tensor')), may hold values from -6 to 6
- segments: int32 [8, 1024], P('dp'), may hold values from 0 to 11, never falling along the last dimension, each value on 1 to 512 neighbouring positions
- ln1_gain: float32 [1024], replicated, may hold values from 0.1 to 1.9
- ln1_bias: float32 [1024], replicated, may hold values from -1.75 to 1.75
- w_query: bfloat16 [1024, 1024], P('dp', 'tensor'), may hold values from -0.25 to 0.25
- b_query: float32 [1024], replicated, may hold values from -3 to 3
- w_key: bfloat16 [1024, 1024], P('dp', 'tensor'), may hold values from -0.25 to 0.25
- w_value: bfloat16 [1024, 1024], P('dp', 'tensor'), may hold values from -0.1875 to 0.1875
- b_value: float32 [1024], replicated, may hold values from -3 to 3
- head_scale: float32 [16], replicated, may hold values from 0.5 to 2
- w_out: bfloat16 [1024, 1024], P('tensor', 'dp'), may hold values from -0.1875 to 0.1875
- b_out: float32 [1024], replicated, may hold values from -3 to 3
- post_gain: float32 [1024], replicated, may hold values from 0.1 to 1.9
- post_bias: float32 [1024], replicated, may hold values from -1.75 to 1.75
- ln2_gain: float32 [1024], replicated, may hold values from 0.1 to 1.9
- ln2_bias: float32 [1024], replicated, may hold values from -1.75 to 1.75
- w_up: bfloat16 [1024, 4096], P('dp', 'tensor'), may hold values from -0.1875 to 0.1875
- b_up: float32 [4096], replicated, may hold values from -3 to 3
- ffn_gain: float32 [4096], replicated, may hold values from 0.1 to 1.9
- ffn_bias: float32 [4096], replicated, may hold values from -1.75 to 1.75
- w_down: bfloat16 [4096, 1024], P('tensor', 'dp'), may hold values from -0.09375 to 0.09375
- b_down: float32 [1024], replicated, may hold values from -1.75 to 1.75
- cotangent: bfloat16 [8192, 1024], P(('dp', 'tensor')), may hold values from -6 to 6
Outputs:
- output: bfloat16 [8192, 1024], P(('dp', 'tensor'))
- input_grad: float32 [8192, 1024], P(('dp', 'tensor'))
- grad_ln1_gain: float32 [1024], replicated
- grad_ln1_bias: float32 [1024], replicated
- grad_w_query: float32 [1024, 1024], P('dp', 'tensor')
- grad_b_query: float32 [1024], replicated
- grad_w_key: float32 [1024, 1024], P('dp', 'tensor')
- grad_w_value: float32 [1024, 1024], P('dp', 'tensor')
- grad_b_value: float32 [1024], replicated
- grad_head_scale: float32 [16], replicated
- grad_w_out: float32 [1024, 1024], P('tensor', 'dp')
- grad_b_out: float32 [1024], replicated
- grad_post_gain: float32 [1024], replicated
- grad_post_bias: float32 [1024], replicated
- grad_ln2_gain: float32 [1024], replicated
- grad_ln2_bias: float32 [1024], replicated
- grad_w_up: float32 [1024, 4096], P('dp', 'tensor')
- grad_b_up: float32 [4096], replicated
- grad_ffn_gain: float32 [4096], replicated
- grad_ffn_bias: float32 [4096], replicated
- grad_w_down: float32 [4096, 1024], P('tensor', 'dp')
- grad_b_down: float32 [1024], replicated
Inputs may be any that keep to these rules, and one draw needn't show every extreme that they name: `segments`: along each sequence segment numbers never fall; a document covers at most 512 positions, and some document covers exactly that many.
All inputs are finite; a program needn't handle non-finite values.
Results may differ from a plain program's by a relative error of at most 0.013.
The roundings to bfloat16 on the way count: a program that leaves them out, or rounds other values in their place, can miss the bound.
Values may be sent and summed in bfloat16 or wider, within the bound.
No kernel may reach another device: no remote copies, remote signals or barrier semaphores. Data moves between devices by JAX's collectives and lax.ppermute only.
A program may use at most 128 MiB of HBM per device.

v0:
```python
import functools

import jax
import jax.numpy as jnp
from jax import lax
from jax.experimental import pallas as pl
from jax.experimental.pallas import tpu as pltpu
from jax.sharding import PartitionSpec as P

D = 1024
HEADS = 16
HD = 64
FF = 4096
LONGEST = 512
EPS = 1e-05
SCALE = HD ** (-0.5)
F32 = jnp.float32
BF16 = jnp.bfloat16


def dot(left, right, left_dim=1, right_dim=0):
    return lax.dot_general(
        left, right, (((left_dim,), (right_dim,)), ((), ())), preferred_element_type=F32
    )


def swap(value, axis, mask):
    size = lax.axis_size(axis)
    return lax.ppermute(value, axis, [(i, i ^ mask) for i in range(size)])


def bit_of(axis, mask):
    return (lax.axis_index(axis) // mask) % 2


def after(value, *others):
    return lax.optimization_barrier((value,) + others)[0]


def row(vector):
    return vector[None, :]


def each_rows(count, step, body):
    def one(k, carry):
        body(pl.ds(pl.multiple_of(k * step, step), step))
        return carry

    lax.fori_loop(0, count // step, one, 0)


STEP = 128


def fold(value):
    return jnp.sum(value.reshape(value.shape[0] // 8, 8, value.shape[1]), axis=0)


def norm_stats(values):
    mean = jnp.mean(values, axis=-1, keepdims=True)
    centered = values - mean
    inverse = lax.rsqrt(jnp.mean(centered * centered, axis=-1, keepdims=True) + EPS)
    return centered * inverse, inverse


def norm_backward(grad, unit, inverse, gain):
    scaled = grad * gain
    return inverse * (
        scaled
        - jnp.mean(scaled, axis=-1, keepdims=True)
        - unit * jnp.mean(scaled * unit, axis=-1, keepdims=True)
    )


VMEM = pl.BlockSpec(memory_space=pltpu.VMEM)
SMEM = pl.BlockSpec(memory_space=pltpu.SMEM)


def shaped(shape, kind):
    return jax.ShapeDtypeStruct(shape, kind)


def cost(flops, moved, hard=0):
    return pl.CostEstimate(flops=flops, bytes_accessed=moved, transcendentals=hard)


class Shards:
    def __init__(self, shard):
        self.held = {0: shard[None]}

    def send(self, mask, *which):
        for k in which:
            self.held[k ^ mask] = swap(self.held[k], "dp", mask)

    def get(self, *which):
        return [self.held[k] for k in which]

    def put(self, which, values):
        for k, value in zip(which, values):
            self.held[k] = value

    def all(self):
        masks = sorted(self.held)
        return [[k] for k in masks], [self.held[k] for k in masks]


def phase(*values):
    return lax.optimization_barrier(values)


def fill(axis, masks, order_ref, piece_refs, full_ref, start=0, width=None):
    if masks is None:
        full_ref[...] = piece_refs[0][...]
        return
    for group, piece in zip(masks, piece_refs):
        height = piece.shape[1]
        for k, mask in enumerate(group):
            place = order_ref[mask]
            if axis == 0:
                there = pl.ds(pl.multiple_of(place * height, height), height)
                full_ref[there, :] = piece[k, :, start : start + full_ref.shape[1]]
            else:
                there = pl.ds(pl.multiple_of(place * width, width), width)
                for low in range(0, full_ref.shape[0], height):
                    at = start + low // height * width
                    full_ref[low : low + height, there] = piece[k, :, at : at + width]


def pack_kernel(q_ref, k_ref, v_ref, o_ref, out_ref):
    height, width = q_ref.shape
    for k, ref in enumerate((q_ref, k_ref, v_ref)):
        out_ref[:, k * width : (k + 1) * width] = ref[...]
    wide = o_ref.shape[1]
    for k in range(o_ref.shape[0] // height):
        at = 3 * width + k * wide
        out_ref[:, at : at + wide] = o_ref[k * height : (k + 1) * height, :]


def pack(w_query, w_key, w_value, w_out):
    height, width = w_query.shape
    total = 3 * width + w_out.size // height
    return pl.pallas_call(
        pack_kernel,
        out_shape=shaped((height, total), BF16),
        in_specs=[VMEM] * 4,
        out_specs=VMEM,
        cost_estimate=cost(0, 0),
        name="pack",
    )(w_query, w_key, w_value, w_out)


def pick_cols(value, width, bit):
    rows, cols = value.shape
    pairs = cols // (2 * width)
    if width % 128:
        return lax.dynamic_index_in_dim(
            value.reshape(rows, pairs, 2, width), bit, 2, keepdims=False
        ).reshape(rows, pairs * width)
    return jnp.concatenate(
        [
            lax.dynamic_slice_in_dim(value, (2 * p + bit) * width, width, 1)
            for p in range(pairs)
        ],
        1,
    )


def pick_rows(value, height, bit):
    rows, cols = value.shape
    return lax.dynamic_index_in_dim(
        value.reshape(rows // (2 * height), 2, height, cols), bit, 1, keepdims=False
    ).reshape(rows // 2, cols)


def dp_masks(last):
    size = lax.axis_size("dp")
    masks = [1 << k for k in range(size.bit_length() - 1)]
    if last in masks:
        masks.remove(last)
        masks.append(last)
    return masks


def outer_kernel(width, on_left, count, bit_ref, *refs):
    parts, (other_ref, send_ref, keep_ref, *picks) = refs[:count], refs[count:]

    @pl.when(pl.program_id(0) == 0)
    def _():
        for bit, pick_ref in zip((1 - bit_ref[0], bit_ref[0]), picks):
            for p in range(pick_ref.shape[1] // width):
                there = pl.ds(pl.multiple_of((2 * p + bit) * width, width), width)
                row = 0
                for part in parts:
                    pick_ref[row : row + part.shape[0], p * width : (p + 1) * width] = part[:, there]
                    row += part.shape[0]

    for pick_ref, out_ref in zip(picks, (send_ref, keep_ref)):
        if on_left:
            value = dot(pick_ref[...], other_ref[...], 0, 0)
        else:
            value = dot(other_ref[...], pick_ref[...], 0, 0)
        out_ref[...] = value.astype(out_ref.dtype)


def outer(bit, picked, other, width, on_left, part, parts):
    rows, cols = other.shape[0], other.shape[1] // parts
    half = picked[0].shape[1] // 2
    step = 256 if cols % 512 == 0 else cols
    skip = part * (cols // step)
    shape = (half, cols) if on_left else (cols, half)
    tile = (half, step) if on_left else (step, half)
    out = pl.BlockSpec(tile, (lambda i: (0, i)) if on_left else (lambda i: (i, 0)))
    return pl.pallas_call(
        functools.partial(outer_kernel, width, on_left, len(picked)),
        grid=(cols // step,),
        out_shape=(shaped(shape, BF16), shaped(shape, F32)),
        in_specs=[SMEM] + [VMEM] * len(picked) + [pl.BlockSpec((rows, step), lambda i: (0, i + skip))],
        out_specs=(out,) * 2,
        scratch_shapes=[pltpu.VMEM((rows, half), BF16)] * 2,
        cost_estimate=cost(0, 0),
        name="outer",
    )(bit, *picked, other)


def split_kernel(axis, width, bit_ref, keep_ref, got_ref, send_ref, stay_ref):
    for bit, out_ref in ((1 - bit_ref[0], send_ref), (bit_ref[0], stay_ref)):
        for p in range(out_ref.shape[axis] // width):
            there = pl.ds(pl.multiple_of((2 * p + bit) * width, width), width)
            here = slice(p * width, (p + 1) * width)
            source, target = ((there, slice(None)), (here, slice(None)))
            if axis == 1:
                source, target = source[::-1], target[::-1]
            value = keep_ref[source] + got_ref[source].astype(F32)
            out_ref[target] = value.astype(out_ref.dtype)


def split(bit, keep, got, width, axis):
    cut = lambda shape: tuple(n // 2 if k == axis else n for k, n in enumerate(shape))
    size = keep.shape[1 - axis]
    step = size // 2 if size % 256 == 0 else size
    tile = tuple(n if k == axis else step for k, n in enumerate(keep.shape))
    index = (lambda i: (0, i)) if axis == 0 else (lambda i: (i, 0))
    return pl.pallas_call(
        functools.partial(split_kernel, axis, width),
        grid=(size // step,),
        out_shape=(shaped(cut(keep.shape), BF16), shaped(cut(keep.shape), F32)),
        in_specs=[SMEM, pl.BlockSpec(tile, index), pl.BlockSpec(tile, index)],
        out_specs=(pl.BlockSpec(cut(tile), index),) * 2,
        cost_estimate=cost(16 * 10**9, 0),
        name="split",
    )(bit, keep, got)


class Scatter:
    def __init__(self, axis, extent, last=0):
        self.axis, self.extent, self.masks = axis, extent, dp_masks(last)

    def place(self):
        mask = self.masks[0]
        lower = sum(1 for other in self.masks if other < mask)
        return bit_of("dp", mask), self.extent << lower

    def product(self, picked, other, part=0, parts=1):
        bit, width = self.place()
        if width % 128 == 0:
            bit = jnp.full((1,), bit, jnp.int32)
            send, self.keep = outer(bit, picked, other, width, self.axis == 0, part, parts)
            return send
        span = other.shape[1] // parts
        other = other[:, part * span : (part + 1) * span]
        picked = jnp.concatenate(picked, 0)
        send, keep = pick_cols(picked, width, 1 - bit), pick_cols(picked, width, bit)
        if self.axis == 0:
            send, self.keep = dot(send, other, 0, 0), dot(keep, other, 0, 0)
        else:
            send, self.keep = dot(other, send, 0, 0), dot(other, keep, 0, 0)
        return send.astype(BF16)

    def start(self, send):
        self.got = swap(send, "dp", self.masks.pop(0))

    def split(self):
        bit, width = self.place()
        if width % 128 == 0:
            send, self.keep = split(jnp.full((1,), bit, jnp.int32), self.keep, self.got, width, self.axis)
            return send
        pick = (pick_rows, pick_cols)[self.axis]
        total = self.keep + self.got.astype(F32)
        self.keep = pick(total, width, bit)
        return pick(total, width, 1 - bit).astype(BF16)

    def finish(self):
        while self.masks:
            self.start(self.split())
        return self.keep + self.got.astype(F32)


def low_kernel(keep_ref, got_ref, out_ref):
    out_ref[...] = (keep_ref[...] + got_ref[...].astype(F32)).astype(BF16)


def low_rows(keep, got, rows):
    total, width = keep.shape
    step = rows // 2
    first = (total - rows) // step
    there = pl.BlockSpec((step, width), lambda i: (i + first, 0))
    return pl.pallas_call(
        low_kernel,
        grid=(rows // step,),
        out_shape=shaped((rows, width), BF16),
        in_specs=[there, there],
        out_specs=pl.BlockSpec((step, width), lambda i: (i, 0)),
        cost_estimate=cost(16 * 10**9, 0),
        name="low_rows",
    )(keep, got)


def stack_kernel(*refs):
    *parts, out_ref = refs
    row = 0
    for part in parts:
        out_ref[row : row + part.shape[0], :] = part[...]
        row += part.shape[0]


def stack(*parts):
    return pl.pallas_call(
        stack_kernel,
        out_shape=shaped((sum(part.shape[0] for part in parts), parts[0].shape[1]), parts[0].dtype),
        in_specs=[VMEM] * len(parts),
        out_specs=VMEM,
        cost_estimate=cost(0, 0),
        name="stack",
    )(*parts)


def project_kernel(inner_ref, weight_ref, send_ref, keep_ref):
    half = inner_ref.shape[0] // 2
    step = half // 2

    def body(rows):
        later = pl.ds(pl.multiple_of(half + rows.start, step), step)
        send_ref[rows, :] = dot(inner_ref[later, :], weight_ref[...]).astype(BF16)
        keep_ref[rows, :] = dot(inner_ref[rows, :], weight_ref[...])

    each_rows(half, step, body)


def project(inner, weight):
    half = inner.shape[0] // 2
    return pl.pallas_call(
        project_kernel,
        out_shape=(shaped((half, D), BF16), shaped((half, D), F32)),
        in_specs=[VMEM] * 2,
        out_specs=(VMEM,) * 2,
        cost_estimate=cost(0, 0),
        name="project",
    )(inner, weight)


def norm_one_kernel(a_ref, b_ref, c_ref, d_ref, gain_ref, bias_ref, out_ref, all_ref, cols_ref):
    step = pl.program_id(0)
    per = pl.num_programs(0) // 4
    value = jnp.where(
        step < 2 * per,
        jnp.where(step < per, a_ref[...], b_ref[...]),
        jnp.where(step < 3 * per, c_ref[...], d_ref[...]),
    )
    all_ref[...] = value
    value = value.astype(F32)
    mean = jnp.mean(value, axis=-1, keepdims=True)
    centered = value - mean
    inverse = lax.rsqrt(jnp.mean(centered * centered, axis=-1, keepdims=True) + EPS)
    lane = lax.broadcasted_iota(jnp.int32, cols_ref.shape, 1)
    cols_ref[...] = jnp.where(lane == 0, mean, inverse)
    out_ref[...] = (centered * inverse * gain_ref[...] + bias_ref[...]).astype(BF16)


def norm_one(parts, gain, bias):
    rows, width = parts[0].shape
    per = rows // STEP

    def spec(first, count, width=width):
        return pl.BlockSpec((STEP, width), lambda i: (jnp.clip(i - first, 0, count - 1), 0))

    return pl.pallas_call(
        norm_one_kernel,
        grid=(4 * per,),
        out_shape=(
            shaped((4 * rows, width), BF16),
            shaped((4 * rows, width), BF16),
            shaped((4 * rows, 128), F32),
        ),
        in_specs=[spec(k * per, per) for k in range(4)] + [VMEM, VMEM],
        out_specs=(spec(0, 4 * per), spec(0, 4 * per), spec(0, 4 * per, 128)),
        cost_estimate=cost(0, 0),
        name="norm_one",
    )(*parts, row(gain), row(bias))


def key_range(block, size):
    low = max(0, block * size - (LONGEST // size) * size)
    return low, (block + 1) * size - low


def write_bias(bias_ref, seg_col_ref, seg_row_ref, rows, keys_at):
    shape = (keys_at.size, rows.size)
    key_pos = keys_at.start + lax.broadcasted_iota(jnp.int32, shape, 0)
    row_pos = rows.start + lax.broadcasted_iota(jnp.int32, shape, 1)
    same = seg_col_ref[keys_at, :] == seg_row_ref[:, rows]
    bias_ref[: keys_at.size, :] = jnp.where((key_pos <= row_pos) & same, 0.0, -1000000000.0)


def each_block(blocks, size, body):
    short = min(LONGEST // size, blocks)
    for block in range(short):
        body(block, *key_range(block, size))

    def one(block, carry):
        low = pl.multiple_of((block - short) * size, size)
        body(block, low, (short + 1) * size)
        return carry

    lax.fori_loop(short, blocks, one, 0)


def attend_kernel(size, masks, place_ref, order_ref, normed_ref, qkv_b_ref, seg_col_ref, seg_row_ref,
                  scale_ref, *refs):
    *pieces, qkv_ref, o_ref, u_ref, lse_ref, qkv_w_ref, out_w_ref, send_ref, keep_ref = refs[:-3]
    bias_ref, vt_ref, ot_ref = refs[-3:]
    length, width = o_ref.shape
    heads = width // HD
    if masks is None:
        qkv_w_ref[...] = pieces[0][...]
        out_w_ref[...] = pieces[1][...]
    else:
        fill(0, masks, order_ref, pieces, qkv_w_ref)
        fill(1, masks, order_ref, pieces, out_w_ref, 3 * width, pieces[0].shape[1])
    head_of = lax.broadcasted_iota(jnp.int32, (size, width), 1) // HD
    def project_block(block, carry):
        rows = pl.ds(pl.multiple_of(block * size, size), size)
        here = pl.ds(pl.multiple_of(place_ref[block] * size, size), size)
        product = dot(normed_ref[here, :], qkv_w_ref[...]) + qkv_b_ref[...]
        qkv_ref[rows, :] = product.astype(BF16)
        vt_ref[:, rows] = product[:, 2 * width :].T.astype(BF16)
        return carry

    def attend_block(block, low, count):
        rows, keys_at = pl.ds(block * size, size), pl.ds(low, count)
        here = pl.ds(pl.multiple_of(place_ref[block] * size, size), size)
        write_bias(bias_ref, seg_col_ref, seg_row_ref, rows, keys_at)
        query = qkv_ref[rows, :width].astype(F32) * SCALE
        keys = qkv_ref[keys_at, width : 2 * width]
        for head in range(heads):
            masked = jnp.where(head_of == head, query, 0.0).astype(BF16)
            scores = dot(keys, masked, 1, 1) + bias_ref[:count, :]
            highest = jnp.max(scores, axis=0, keepdims=True)
            raised = jnp.exp(scores - highest)
            total = jnp.sum(raised, axis=0, keepdims=True)
            lse_ref[block, head : head + 1, :] = highest + jnp.log(total)
            probs = (raised * (1.0 / total)).astype(BF16)
            part = slice(head * HD, (head + 1) * HD)
            ot_ref[part, :] = dot(vt_ref[part, keys_at], probs)
        mixed = ot_ref[...].T
        o_ref[rows, :] = mixed
        u_ref[here, :] = (mixed * scale_ref[...]).astype(BF16)

    lax.fori_loop(0, length // size, project_block, 0)
    each_block(length // size, size, attend_block)
    half = length // 2
    send_ref[...] = dot(u_ref[half:, :], out_w_ref[...]).astype(BF16)
    keep_ref[...] = dot(u_ref[:half, :], out_w_ref[...])


def attend_back_kernel(size, place_ref, qkv_ref, own_ref, rest_ref, out_w_ref, o_ref, lse_ref,
                       seg_col_ref, seg_row_ref, scale_ref, dqkv_ref, sums_ref,
                       bias_ref, kt_ref, dqt_ref, probs_ref, ds_ref, q_ref, do_ref, dk_ref, dv_ref,
                       du_ref, acc_ref):
    length, width = o_ref.shape
    heads = width // HD
    du_ref[: length // 2, :] = dot(own_ref[...], out_w_ref[...], 1, 1)
    du_ref[length // 2 :, :] = dot(rest_ref[...], out_w_ref[...], 1, 1)
    kt_ref[...] = qkv_ref[:, width : 2 * width].astype(F32).T.astype(BF16)
    head_of = lax.broadcasted_iota(jnp.int32, (size, width), 1) // HD
    blocks = length // size
    acc_ref[...] = jnp.zeros_like(acc_ref)

    def back_block(block, low, count):
        rows, keys_at = pl.ds(block * size, size), pl.ds(low, count)
        here = pl.ds(pl.multiple_of(place_ref[block] * size, size), size)
        write_bias(bias_ref, seg_col_ref, seg_row_ref, rows, keys_at)
        query = qkv_ref[rows, :width].astype(F32) * SCALE
        keys = qkv_ref[keys_at, width : 2 * width]
        values = qkv_ref[keys_at, 2 * width :]
        du = du_ref[here, :]
        acc_ref[0:8, :] += fold(du * o_ref[rows, :])
        grad = du * scale_ref[...]
        for head in range(heads):
            masked = jnp.where(head_of == head, query, 0.0).astype(BF16)
            grad_here = jnp.where(head_of == head, grad, 0.0).astype(BF16)
            stack = slice(head * size, (head + 1) * size)
            q_ref[stack, :] = masked
            do_ref[stack, :] = grad_here
            scores = dot(keys, masked, 1, 1) + bias_ref[:count, :]
            full = jnp.exp(scores - lse_ref[block, head : head + 1, :])
            probs_ref[:count, stack] = full.astype(BF16)
            dp = dot(values, grad_here, 1, 1)
            delta = jnp.sum(full * dp, axis=0, keepdims=True)
            ds = (full * (dp - delta)).astype(BF16)
            ds_ref[:count, stack] = ds
            part = slice(head * HD, (head + 1) * HD)
            dqt_ref[part, :] = dot(kt_ref[part, keys_at], ds)
        dq = (dqt_ref[...].T * SCALE).astype(BF16)
        dqkv_ref[here, :width] = dq
        acc_ref[8:16, :] += fold(dq.astype(F32))
        dk = dot(ds_ref[:count, :], q_ref[...])
        dv = dot(probs_ref[:count, :], do_ref[...])
        old = count - size
        if old:
            before = pl.ds(low, old)
            dk_ref[before, :] += dk[:old]
            dv_ref[before, :] += dv[:old]
        dk_ref[rows, :] = dk[old:]
        dv_ref[rows, :] = dv[old:]

    each_block(blocks, size, back_block)

    def finish_block(block, carry):
        rows = pl.ds(pl.multiple_of(block * size, size), size)
        here = pl.ds(pl.multiple_of(place_ref[block] * size, size), size)
        dqkv_ref[here, width : 2 * width] = dk_ref[rows, :].astype(BF16)
        dv = dv_ref[rows, :].astype(BF16)
        dqkv_ref[here, 2 * width :] = dv
        acc_ref[16:24, :] += fold(dv.astype(F32))
        return carry

    lax.fori_loop(0, blocks, finish_block, 0)
    sums_ref[...] = jnp.concatenate(
        [jnp.sum(acc_ref[8 * k : 8 * k + 8, :], axis=0, keepdims=True) for k in (1, 2, 0)]
        + [jnp.zeros((5, width), F32)],
        axis=0,
    )


def attend(place, order, normed, masks, pieces, qkv_b, seg_col, seg_row, scale_row):
    length, width = normed.shape[0], scale_row.shape[1]
    size = length // 4
    heads = width // HD
    most = LONGEST + size
    return pl.pallas_call(
        functools.partial(attend_kernel, size, masks),
        out_shape=(
            shaped((length, 3 * width), BF16),
            shaped((length, width), F32),
            shaped((length, width), BF16),
            shaped((4, heads, size), F32),
            shaped((D, 3 * width), BF16),
            shaped((width, D), BF16),
            shaped((length // 2, D), BF16),
            shaped((length // 2, D), F32),
        ),
        in_specs=[SMEM] * 2 + [VMEM] * (5 + len(pieces)),
        out_specs=(VMEM,) * 8,
        scratch_shapes=[
            pltpu.VMEM((most, size), F32),
            pltpu.VMEM((width, length), BF16),
            pltpu.VMEM((width, size), F32),
        ],
        cost_estimate=cost(0, 0),
        name="attend",
    )(place, order, normed, qkv_b, seg_col, seg_row, scale_row, *pieces)


def attend_back(place, qkv, own, rest, out_w, mixed, lse, seg_col, seg_row, scale_row):
    length, width = mixed.shape
    size = length // 4
    heads = width // HD
    most = LONGEST + size
    pairs = 4 * heads * most * size
    return pl.pallas_call(
        functools.partial(attend_back_kernel, size),
        out_shape=(shaped((length, 3 * width), BF16), shaped((8, width), F32)),
        in_specs=[SMEM] + [VMEM] * 9,
        out_specs=(VMEM,) * 2,
        scratch_shapes=[
            pltpu.VMEM((most, size), F32),
            pltpu.VMEM((width, length), BF16),
            pltpu.VMEM((width, size), F32),
            pltpu.VMEM((most, heads * size), BF16),
            pltpu.VMEM((most, heads * size), BF16),
            pltpu.VMEM((heads * size, width), BF16),
            pltpu.VMEM((heads * size, width), BF16),
            pltpu.VMEM((length, width), F32),
            pltpu.VMEM((length, width), F32),
            pltpu.VMEM((length, width), F32),
            pltpu.VMEM((24, width), F32),
        ],
        cost_estimate=cost(16 * 10**9, 0),
        name="attend_back",
    )(place, qkv, own, rest, out_w, mixed, lse, seg_col, seg_row, scale_row)


def middle_kernel(keep_ref, got_ref, other_ref, mine_ref, pair_ref, b_out_ref, post_g_ref, post_b_ref,
                  ln2_g_ref, ln2_b_ref, ffn_in_ref, unit2_ref, cols_ref):
    first = pl.program_id(0) < pl.num_programs(0) // 2
    tokens = jnp.where(first, mine_ref[...], pair_ref[...]).astype(F32)
    part = keep_ref[...] + got_ref[...].astype(F32)
    projected = part + other_ref[...].astype(F32) + b_out_ref[...]
    unit2, inv2 = norm_stats(projected)
    unit2_ref[...] = unit2
    hidden = tokens + (unit2 * post_g_ref[...] + post_b_ref[...])
    mean3 = jnp.mean(hidden, axis=-1, keepdims=True)
    centered = hidden - mean3
    inv3 = lax.rsqrt(jnp.mean(centered * centered, axis=-1, keepdims=True) + EPS)
    ffn_in_ref[...] = (centered * inv3 * ln2_g_ref[...] + ln2_b_ref[...]).astype(BF16)
    lane = lax.broadcasted_iota(jnp.int32, cols_ref.shape, 1)
    cols_ref[...] = jnp.where(lane == 0, inv2, jnp.where(lane == 1, mean3, inv3))


def pair_specs(rows, width):
    half = rows // 2 // STEP
    straight = pl.BlockSpec((STEP, width), lambda i: (i, 0))
    crossed = pl.BlockSpec((STEP, width), lambda i: ((i + half) % (2 * half), 0))
    mine = pl.BlockSpec((STEP, width), lambda i: (jnp.minimum(i, half - 1), 0))
    theirs = pl.BlockSpec((STEP, width), lambda i: (jnp.maximum(i - half, 0), 0))
    return straight, crossed, mine, theirs


def middle(keep, got, other, mine, pair, b_out, post_gain, post_bias, ln2_gain, ln2_bias):
    rows, width = keep.shape
    straight, crossed, own, theirs = pair_specs(rows, width)
    columns = pl.BlockSpec((STEP, 128), lambda i: (i, 0))
    return pl.pallas_call(
        middle_kernel,
        grid=(rows // STEP,),
        out_shape=(
            shaped((rows, width), BF16),
            shaped((rows, width), F32),
            shaped((rows, 128), F32),
        ),
        in_specs=[straight, straight, crossed, own, theirs] + [VMEM] * 5,
        out_specs=(straight, straight, columns),
        cost_estimate=cost(0, 0),
        name="middle",
    )(keep, got, other, mine, pair, row(b_out), row(post_gain), row(post_bias), row(ln2_gain),
      row(ln2_bias))


def middle_back_kernel(keep_ref, got_ref, other_ref, mine_ref, pair_ref, tokens_ref, tokens2_ref,
                       unit2_ref, cols_ref, post_g_ref, post_b_ref, ln2_g_ref, proj_ref, grad_ref, sums_ref,
                       acc_ref):
    step = pl.program_id(0)
    half = pl.num_programs(0) // 2
    first = step < half

    @pl.when(step == 0)
    def _():
        acc_ref[...] = jnp.zeros_like(acc_ref)

    part = keep_ref[...] + got_ref[...].astype(F32)
    incoming = part + other_ref[...].astype(F32)
    tokens = jnp.where(first, tokens_ref[...], tokens2_ref[...]).astype(F32)
    unit2 = unit2_ref[...]
    inv2, mean3, inv3 = (cols_ref[:, k : k + 1] for k in range(3))
    hidden = tokens + (unit2 * post_g_ref[...] + post_b_ref[...])
    unit3 = (hidden - mean3) * inv3
    outgoing = jnp.where(first, mine_ref[...], pair_ref[...]).astype(F32)
    grad = outgoing + norm_backward(incoming, unit3, inv3, ln2_g_ref[...])
    proj = norm_backward(grad, unit2, inv2, post_g_ref[...]).astype(BF16)
    proj_ref[...] = proj

    @pl.when(first)
    def _():
        grad_ref[...] = grad
        for k, value in enumerate(
            (incoming * unit3, incoming, grad * unit2, grad, proj.astype(F32), outgoing)
        ):
            acc_ref[8 * k : 8 * k + 8, :] += fold(value)

    @pl.when(step == half - 1)
    def _():
        sums_ref[...] = jnp.concatenate(
            [jnp.sum(acc_ref[8 * k : 8 * k + 8, :], axis=0, keepdims=True) for k in range(6)]
            + [jnp.zeros((2, acc_ref.shape[1]), F32)],
            axis=0,
        )


def middle_back(keep, got, other, mine, pair, tokens, tokens2, unit2, cols, post_gain, post_bias,
                ln2_gain):
    rows, width = keep.shape
    straight, crossed, own, theirs = pair_specs(rows, width)
    columns = pl.BlockSpec((STEP, 128), lambda i: (i, 0))
    return pl.pallas_call(
        middle_back_kernel,
        grid=(rows // STEP,),
        out_shape=(
            shaped((rows, width), BF16),
            shaped((rows // 2, width), F32),
            shaped((8, width), F32),
        ),
        in_specs=[straight, straight, crossed, own, theirs, own, theirs, straight, columns] + [VMEM] * 3,
        out_specs=(straight, own, VMEM),
        scratch_shapes=[pltpu.VMEM((48, width), F32)],
        cost_estimate=cost(0, 0),
        name="middle_back",
    )(keep, got, other, mine, pair, tokens, tokens2, unit2, cols, row(post_gain), row(post_bias),
      row(ln2_gain))


def ffn_one_kernel(masks, order_ref, in_ref, b_up_ref, *refs):
    *pieces, active_ref, slope_ref, stats_ref, up_ref, cols_ref = refs

    @pl.when(pl.program_id(0) == 0)
    def _():
        fill(0, masks, order_ref, pieces, up_ref)

    active_ref[...] = dot(in_ref[...], up_ref[...]) + b_up_ref[...]
    lane = lax.broadcasted_iota(jnp.int32, (STEP, 128), 1)

    def body(rows):
        before = active_ref[rows, :]
        cdf = 0.5 * (1.0 + lax.erf(before * 0.7071067811865476))
        active = before * cdf
        density = jnp.exp(-0.5 * before * before) * 0.3989422804014327
        slope_ref[rows, :] = cdf + before * density
        active_ref[rows, :] = active
        mean = jnp.mean(active, axis=-1, keepdims=True)
        off = active - mean
        square = jnp.sum(off * off, axis=-1, keepdims=True)
        cols_ref[rows, :] = jnp.where(lane == 0, mean, square)

    each_rows(active_ref.shape[0], STEP, body)
    stats_ref[...] = cols_ref[...].T[:8, :]


def ffn_one(ffn_in, order, masks, pieces, b_up):
    rows, width = ffn_in.shape[0], b_up.shape[0]
    size = 256
    tile = pl.BlockSpec((size, width), lambda i: (i, 0))
    return pl.pallas_call(
        functools.partial(ffn_one_kernel, masks),
        grid=(rows // size,),
        out_shape=(
            shaped((rows, width), F32),
            shaped((rows, width), F32),
            shaped((8, rows), F32),
            shaped((D, width), BF16),
        ),
        in_specs=[SMEM, pl.BlockSpec((size, D), lambda i: (i, 0)), VMEM] + [VMEM] * len(pieces),
        out_specs=(tile, tile, pl.BlockSpec((8, size), lambda i: (0, i)), VMEM),
        scratch_shapes=[pltpu.VMEM((size, 128), F32)],
        cost_estimate=cost(0, 0),
        name="ffn_one",
    )(order, ffn_in, row(b_up), *pieces)


def ffn_grad_kernel(masks, order_ref, grad_ref, keep_ref, send_ref, stats_k_ref, stats_s_ref, gain_ref,
                    *refs):
    *pieces, inner_ref, stats_ref, down_ref, cols_ref = refs
    step = pl.program_id(0)
    first = step < pl.num_programs(0) // 2

    @pl.when(step == 0)
    def _():
        fill(1, masks, order_ref, pieces, down_ref, 0, pieces[0].shape[-1])

    inner_ref[...] = dot(grad_ref[...], down_ref[...], 1, 1)
    lane = lax.broadcasted_iota(jnp.int32, (STEP, 128), 1)

    def body(rows):
        active = jnp.where(first, keep_ref[rows, :], send_ref[rows, :])
        scaled = inner_ref[rows, :] * gain_ref[...]
        plain = jnp.sum(scaled, axis=-1, keepdims=True)
        cross = jnp.sum(scaled * active, axis=-1, keepdims=True)
        cols_ref[rows, :] = jnp.where(lane == 2, plain, cross)

    each_rows(inner_ref.shape[0], STEP, body)
    stats = jnp.where(first, stats_k_ref[...], stats_s_ref[...])
    index = lax.broadcasted_iota(jnp.int32, stats.shape, 0)
    stats_ref[...] = jnp.where(index < 2, stats, cols_ref[...].T[:8, :])


def ffn_grad(grad, order, masks, pieces, active_k, active_s, stats_k, stats_s, gain):
    rows, width = grad.shape[0], gain.shape[0]
    size = 256
    half = rows // size // 2
    keep = lambda i: jnp.minimum(i, half - 1)
    send = lambda i: jnp.maximum(i - half, 0)
    tile = (size, width)
    return pl.pallas_call(
        functools.partial(ffn_grad_kernel, masks),
        grid=(rows // size,),
        out_shape=(
            shaped((rows, width), F32),
            shaped((8, rows), F32),
            shaped((width, D), BF16),
        ),
        in_specs=[
            SMEM,
            pl.BlockSpec((size, D), lambda i: (i, 0)),
            pl.BlockSpec(tile, lambda i: (keep(i), 0)),
            pl.BlockSpec(tile, lambda i: (send(i), 0)),
            pl.BlockSpec((8, size), lambda i: (0, keep(i))),
            pl.BlockSpec((8, size), lambda i: (0, send(i))),
            VMEM,
        ]
        + [VMEM] * len(pieces),
        out_specs=(
            pl.BlockSpec(tile, lambda i: (i, 0)),
            pl.BlockSpec((8, size), lambda i: (0, i)),
            VMEM,
        ),
        scratch_shapes=[pltpu.VMEM((size, 128), F32)],
        cost_estimate=cost(0, 0),
        name="ffn_grad",
    )(order, grad, active_k, active_s, stats_k, stats_s, row(gain), *pieces)


def ffn_two_kernel(mk_ref, ms_ref, sk_ref, ss_ref, grad_ref, s0_ref, s1_ref, s2_ref, s3_ref, gain_ref,
                   shift_ref, up_ref, inner_ref, before_ref, send_ref, keep_ref, sums_ref, cols_ref,
                   acc_ref):
    step = pl.program_id(0)
    half = pl.num_programs(0) // 2
    count, width = inner_ref.shape

    @pl.when(step == 0)
    def _():
        acc_ref[...] = jnp.zeros_like(acc_ref)

    values = [ref[...] for ref in (s0_ref, s1_ref, s2_ref, s3_ref)]
    mean = 0.25 * ((values[0][0:1] + values[1][0:1]) + (values[2][0:1] + values[3][0:1]))
    square = plain = cross = jnp.zeros_like(mean)
    for value in values:
        gap = value[0:1] - mean
        square = square + (value[1:2] + width * (gap * gap))
        plain = plain + value[2:3]
        cross = cross + value[3:4]
    inverse = lax.rsqrt(square / FF + EPS)
    cross = (cross - mean * plain) * inverse
    table = jnp.concatenate(
        [mean, inverse, plain / FF, cross / FF, jnp.zeros((124, count), F32)], axis=0
    )
    cols_ref[...] = table.T

    def work(active_ref, slope_ref, out_ref):
        def body(rows):
            cols = cols_ref[rows, :]
            mean, inverse, plain, cross = (cols[:, k : k + 1] for k in range(4))
            unit = (active_ref[rows, :] - mean) * inverse
            inner_ref[rows, :] = (unit * gain_ref[...] + shift_ref[...]).astype(BF16)
            grad = grad_ref[rows, :]
            moved = inverse * (grad * gain_ref[...] - plain - unit * cross)
            before = (moved * slope_ref[rows, :]).astype(BF16)
            before_ref[rows, :] = before
            for k, value in enumerate((before.astype(F32), grad * unit, grad)):
                acc_ref[8 * k : 8 * k + 8, :] += fold(value)

        each_rows(count, STEP, body)
        out_ref[...] = dot(before_ref[...], up_ref[...], 1, 1).astype(out_ref.dtype)

    @pl.when(step < half)
    def _():
        work(ms_ref, ss_ref, send_ref)

    @pl.when(step >= half)
    def _():
        work(mk_ref, sk_ref, keep_ref)

    @pl.when(step == 2 * half - 1)
    def _():
        sums_ref[...] = jnp.concatenate(
            [jnp.sum(acc_ref[8 * k : 8 * k + 8, :], axis=0, keepdims=True) for k in range(3)]
            + [jnp.zeros((5, width), F32)],
            axis=0,
        )


def ffn_two(active_k, active_s, slope_k, slope_s, inner_grad, stats, gain, shift, up_w):
    rows, width = active_k.shape
    size = 256
    half = rows // size
    keep = lambda i: jnp.maximum(i - half, 0)
    send = lambda i: jnp.minimum(i, half - 1)
    keep_spec = lambda shape: pl.BlockSpec(shape, lambda i: (keep(i), 0))
    send_spec = lambda shape: pl.BlockSpec(shape, lambda i: (send(i), 0))
    tile = (size, width)
    block = lambda i: (i + half) % (2 * half)
    both = pl.BlockSpec(tile, lambda i: (block(i), 0))
    held = (lambda b: b, lambda b: (b + 2) % 4, lambda b: b + 1 - 2 * (b % 2), lambda b: 3 - b)
    return pl.pallas_call(
        ffn_two_kernel,
        grid=(2 * half,),
        out_shape=(
            shaped((2 * rows, width), BF16),
            shaped((2 * rows, width), BF16),
            shaped((rows, D), BF16),
            shaped((rows, D), F32),
            shaped((8, width), F32),
        ),
        in_specs=[keep_spec(tile), send_spec(tile), keep_spec(tile), send_spec(tile), both]
        + [pl.BlockSpec((8, size), lambda i, at=at: (0, at(block(i)))) for at in held]
        + [VMEM] * 3,
        out_specs=(both, both, send_spec((size, D)), keep_spec((size, D)), VMEM),
        scratch_shapes=[pltpu.VMEM((size, 128), F32), pltpu.VMEM((24, width), F32)],
        cost_estimate=cost(0, 0),
        name="ffn_two",
    )(active_k, active_s, slope_k, slope_s, inner_grad, *stats, row(gain), row(shift), up_w)


def normed_grad_kernel(side_ref, grad_ref, weight_ref, all_ref, cols_ref, sums_ref, middle_ref, ffn_ref,
                       send_ref, keep_ref, late_ref, acc_ref):
    step = pl.program_id(0)
    half = pl.num_programs(0) // 2
    width = late_ref.shape[1]

    @pl.when(step == 0)
    def _():
        acc_ref[...] = jnp.zeros_like(acc_ref)

    grad = dot(grad_ref[...], weight_ref[...], 1, 1)
    unit = (all_ref[...].astype(F32) - cols_ref[:, 0:1]) * cols_ref[:, 1:2]
    for k, value in enumerate((grad * unit, grad)):
        acc_ref[8 * k : 8 * k + 8, :] += fold(value)

    @pl.when(step < half)
    def _():
        send_ref[...] = grad.astype(BF16)

    @pl.when(step >= half)
    def _():
        keep_ref[...] = grad

    @pl.when(step == 2 * half - 1)
    def _():
        here = side_ref[0]
        wide = [
            jnp.concatenate(
                [jnp.where(here == k, sums_ref[r : r + 1, :], 0.0) for k in range(4)], axis=1
            )
            for r in range(3)
        ]
        place = lax.broadcasted_iota(jnp.int32, (4, width), 0) == here
        late_ref[...] = jnp.concatenate(
            [jnp.sum(acc_ref[8 * k : 8 * k + 8, :], axis=0, keepdims=True) for k in range(2)]
            + wide
            + [middle_ref[0:6, :], jnp.zeros((1, width), F32)]
            + [jnp.where(place, ffn_ref[k : k + 1, :], 0.0) for k in range(3)],
            axis=0,
        )


def normed_grad(here, grad_qkv, qkv_w, x_all, cols, sums, middle_sums, ffn_sums):
    length, width = x_all.shape
    size = 256
    half = length // size // 2
    block = lambda i: ((i + half) % (2 * half), 0)
    return pl.pallas_call(
        normed_grad_kernel,
        grid=(2 * half,),
        out_shape=(
            shaped((length // 2, width), BF16),
            shaped((length // 2, width), F32),
            shaped((24, width), F32),
        ),
        in_specs=[
            SMEM,
            pl.BlockSpec((size, grad_qkv.shape[1]), block),
            VMEM,
            pl.BlockSpec((size, width), block),
            pl.BlockSpec((size, 128), block),
            VMEM,
            VMEM,
            VMEM,
        ],
        out_specs=(
            pl.BlockSpec((size, width), lambda i: (jnp.minimum(i, half - 1), 0)),
            pl.BlockSpec((size, width), lambda i: (jnp.maximum(i - half, 0), 0)),
            VMEM,
        ),
        scratch_shapes=[pltpu.VMEM((16, width), F32)],
        cost_estimate=cost(0, 0),
        name="normed_grad",
    )(here, grad_qkv, qkv_w, x_all, cols, sums, middle_sums, ffn_sums)


def last_kernel(keep_ref, got_ref, other_ref, tokens_ref, cols_ref, gain_ref, hidden_ref, grad_ref):
    incoming = keep_ref[...] + got_ref[...].astype(F32) + other_ref[...].astype(F32)
    inverse = cols_ref[:, 1:2]
    unit = (tokens_ref[...].astype(F32) - cols_ref[:, 0:1]) * inverse
    grad_ref[...] = hidden_ref[...] + norm_backward(incoming, unit, inverse, gain_ref[...])


def last(keep, got, other, tokens, cols, gain, grad_hidden):
    rows, width = tokens.shape
    tile = pl.BlockSpec((STEP, width), lambda i: (i, 0))
    return pl.pallas_call(
        last_kernel,
        grid=(rows // STEP,),
        out_shape=shaped((rows, width), F32),
        in_specs=[tile] * 4 + [pl.BlockSpec((STEP, 128), lambda i: (i, 0)), VMEM, tile],
        out_specs=tile,
        cost_estimate=cost(0, 0),
        name="last",
    )(keep, got, other, tokens, cols, row(gain), grad_hidden)


def output_kernel(keep_ref, got_ref, other_ref, tokens_ref, unit2_ref, post_g_ref, post_b_ref, b_down_ref,
                  out_ref):
    hidden = tokens_ref[...].astype(F32) + (unit2_ref[...] * post_g_ref[...] + post_b_ref[...])
    branch = keep_ref[...] + got_ref[...].astype(F32) + other_ref[...].astype(F32)
    out_ref[...] = (hidden + (branch + b_down_ref[...])).astype(BF16)


def output_rows(keep, got, other, tokens, unit2, post_gain, post_bias, b_down):
    rows, width = tokens.shape
    tile = pl.BlockSpec((STEP, width), lambda i: (i, 0))
    return pl.pallas_call(
        output_kernel,
        grid=(rows // STEP,),
        out_shape=shaped((rows, width), BF16),
        in_specs=[tile] * 5 + [VMEM] * 3,
        out_specs=tile,
        cost_estimate=cost(0, 0),
        name="output_rows",
    )(keep, got, other, tokens, unit2, row(post_gain), row(post_bias), row(b_down))


def per_device(
    tokens,
    segments,
    ln1_gain,
    ln1_bias,
    w_query,
    b_query,
    w_key,
    w_value,
    b_value,
    head_scale,
    w_out,
    b_out,
    post_gain,
    post_bias,
    ln2_gain,
    ln2_bias,
    w_up,
    b_up,
    ffn_gain,
    ffn_bias,
    w_down,
    b_down,
    cotangent,
):
    index = lax.axis_index("tensor")
    rows = tokens.shape[0]
    two = 2 * rows
    columns = w_query.shape[1]
    hidden_here = w_up.shape[1]
    shard = D // lax.axis_size("dp")
    order = jnp.array([0, 2, 1, 3], jnp.int32)
    place = order[jnp.arange(4, dtype=jnp.int32) ^ index]
    here = jnp.full((1,), index, jnp.int32)

    def own_part(vector, width):
        return lax.dynamic_slice_in_dim(vector, index * width, width, 0)

    segment = segments[0]
    seg_col, seg_row = segment[:, None], segment[None, :]
    scale_row = row(jnp.repeat(own_part(head_scale, columns // HD), HD))
    qkv_b = jnp.concatenate(
        [own_part(b_query, columns), jnp.zeros((columns,), F32), own_part(b_value, columns)]
    )
    gain_here, shift_here = own_part(ffn_gain, hidden_here), own_part(ffn_bias, hidden_here)
    b_up_here = own_part(b_up, hidden_here)

    order_dp = lax.axis_index("dp") ^ jnp.arange(lax.axis_size("dp"), dtype=jnp.int32)
    quick = shard % 128 == 0 and lax.axis_size("dp") == 8

    attn = None
    if quick:
        packed, tokens = phase(pack(w_query, w_key, w_value, w_out), tokens)
        attn = Shards(packed)
        attn.send(4, 0)
        attn.send(1, 0)
        first = attn.get(4, 1)
    else:
        first = []
        attn_full = [
            lax.all_gather(jnp.concatenate([w_query, w_key, w_value], 1), "dp", axis=0, tiled=True),
            lax.all_gather(w_out, "dp", axis=1, tiled=True),
        ]
        up_full = [lax.all_gather(w_up, "dp", axis=0, tiled=True)]
        down_full = [lax.all_gather(w_down, "dp", axis=1, tiled=True)]
        attn_masks = up_masks = down_masks = None
    x_pair = swap(tokens, "tensor", 2)
    x_side = swap(tokens, "tensor", 1)
    up_s, down_s = Shards(w_up), Shards(w_down)
    own_up, own_down = up_s.held[0], down_s.held[0]
    (x_pair, x_side, own_up, own_down, cotangent, b_up_here, gain_here, shift_here, qkv_b, scale_row,
     seg_col, place, order_dp), first = phase(
        (x_pair, x_side, own_up, own_down, cotangent, b_up_here, gain_here, shift_here, qkv_b,
         scale_row, seg_col, place, order_dp), first)
    if quick:
        attn.put([4, 1], first)

    x_cross = swap(x_pair, "tensor", 1)
    if quick:
        attn.send(2, 0, 4)
        attn.send(1, 4)
        first = attn.get(2, 6, 5)
    g_pair = swap(cotangent, "tensor", 2)
    normed, x_all, cols1 = norm_one([tokens, x_pair, x_side, x_cross], ln1_gain, ln1_bias)
    (normed, x_all, cols1, own_up, own_down, g_pair, cotangent), first = phase(
        (normed, x_all, cols1, own_up, own_down, g_pair, cotangent), first)

    if quick:
        attn.put([2, 6, 5], first)
        attn.send(1, 2, 6)
        up_s.put([0], [own_up])
        up_s.send(4, 0)
        attn_masks, attn_full = attn.all()
        first = up_s.get(4)
    g_side = swap(cotangent, "tensor", 1)
    g_cross = swap(g_pair, "tensor", 1)
    (normed, own_down, own_up, g_side, g_cross), attn_full, first = phase(
        (normed, own_down, own_up, g_side, g_cross), attn_full, first)

    if quick:
        up_s.put([0, 4], [own_up] + first)
        up_s.send(2, 0, 4)
        up_s.send(1, 0, 4)
        first = up_s.get(2, 6, 1, 5)
    qkv, mixed, scaled, lse, qkv_w, out_w, send, keep = attend(
        place, order_dp, normed, attn_masks, attn_full, row(qkv_b), seg_col, seg_row, scale_row
    )
    (qkv, mixed, scaled, lse, qkv_w, out_w, send, keep, own_down, g_side, g_cross), first = phase(
        (qkv, mixed, scaled, lse, qkv_w, out_w, send, keep, own_down, g_side, g_cross), first)

    got = swap(send, "tensor", 1)
    if quick:
        up_s.put([2, 6, 1, 5], first)
        up_s.send(1, 2, 6)
        down_s.put([0], [own_down])
        down_s.send(4, 0)
        first = up_s.get(3, 7) + down_s.get(4)
    low, got, keep, g_side = phase(low_rows(keep, got, two), got, keep, g_side)
    other = swap(low, "tensor", 2)
    (g_all, own_down), first = phase((stack(cotangent, g_pair, g_side, g_cross), own_down), first)
    if quick:
        up_s.put([3, 7], first[:2])
        down_s.put([0, 4], [own_down, first[2]])
        down_s.send(2, 0, 4)
        down_s.send(1, 0, 4)
        other, keep, got = phase(other, keep, got)
        up_masks, up_full = up_s.all()
        first = down_s.get(2, 6, 1, 5)

    ffn_in, unit2, cols = middle(
        keep, got, other, tokens, x_pair, b_out, post_gain, post_bias, ln2_gain, ln2_bias
    )
    (ffn_in, unit2, cols), first = phase((ffn_in, unit2, cols), first)
    ffn_rest = swap(ffn_in, "tensor", 1)
    if quick:
        down_s.put([2, 6, 1, 5], first)
        down_s.send(1, 2, 6)
        down_masks, down_full = down_s.all()
    active_k, slope_k, stats_k, up_w = ffn_one(ffn_in, order_dp, up_masks, up_full, b_up_here)
    active_k, slope_k, stats_k, up_w, ffn_rest = phase(active_k, slope_k, stats_k, up_w, ffn_rest)
    active_s, slope_s, stats_s, _ = ffn_one(ffn_rest, order_dp, None, [up_w], b_up_here)
    (active_s, stats_s, slope_s), down_full = phase((active_s, stats_s, slope_s), down_full)
    inner_grad, stats, down_w = ffn_grad(
        g_all, order_dp, down_masks, down_full, active_k, active_s, stats_k, stats_s, gain_here
    )
    stats = [stats] + [swap(stats, "tensor", mask) for mask in (1, 2, 3)]
    inner, grad_before, send, keep, ffn_sums = ffn_two(
        active_k, active_s, slope_k, slope_s, inner_grad, stats, gain_here, shift_here, up_w
    )

    down_g, up_g, out_g = Scatter(1, shard, 1), Scatter(0, shard), Scatter(1, shard)
    qkv_a, qkv_b = Scatter(0, shard), Scatter(0, shard)
    got = swap(send, "tensor", 1)
    down_send = down_g.product([g_all], inner)
    down_send, down_g.keep, inner, grad_before, got, keep = phase(
        down_send, down_g.keep, inner, grad_before, got, keep
    )
    low, down_send, inner, grad_before = phase(low_rows(keep, got, two), down_send, inner, grad_before)
    other = swap(low, "tensor", 2)
    down_g.start(down_send)
    up_send = up_g.product([ffn_in, ffn_rest], grad_before)
    up_send, up_g.keep, inner = phase(up_send, up_g.keep, inner)
    up_g.start(up_send)
    out_send, out_keep = project(inner, down_w)
    other, down_g.got, out_send, out_keep = phase(other, down_g.got, out_send, out_keep)

    down_send = down_g.split()
    down_send, down_g.keep, other, out_send = phase(down_send, down_g.keep, other, out_send)
    down_g.start(down_send)
    out_got = swap(out_send, "tensor", 1)
    grad_proj, grad_hidden, middle_sums = middle_back(
        keep, got, other, cotangent, g_pair, tokens, x_pair, unit2, cols, post_gain, post_bias,
        ln2_gain,
    )
    grad_proj, up_g.got, out_got, out_keep = phase(grad_proj, up_g.got, out_got, out_keep)
    proj_rest = swap(grad_proj, "tensor", 1)
    up_send = up_g.split()
    out_low = low_rows(out_keep, out_got, rows)
    grad_proj, proj_rest, up_send, up_g.keep, out_low = phase(
        grad_proj, proj_rest, up_send, up_g.keep, out_low
    )
    w_send = out_g.product([grad_proj, proj_rest], scaled)
    w_send, out_g.keep, grad_proj, proj_rest, up_send, out_low = phase(
        w_send, out_g.keep, grad_proj, proj_rest, up_send, out_low
    )

    up_g.start(up_send)
    out_other = swap(out_low, "tensor", 2)
    out_g.start(w_send)
    grad_qkv, sums = attend_back(
        place, qkv, grad_proj, proj_rest, out_w, mixed, lse, seg_col, seg_row, scale_row
    )
    grad_qkv, sums, up_g.got, out_other, out_g.got = phase(
        grad_qkv, sums, up_g.got, out_other, out_g.got
    )

    masks = dp_masks(0)
    up_send, w_send = up_g.split(), out_g.split()
    up_send, up_g.keep, grad_qkv, w_send, out_g.keep = phase(
        up_send, up_g.keep, grad_qkv, w_send, out_g.keep
    )
    up_g.start(up_send)
    out_g.start(w_send)
    a_send = qkv_a.product([normed], grad_qkv, 0, 2)
    a_send, qkv_a.keep, grad_qkv = phase(a_send, qkv_a.keep, grad_qkv)
    qkv_a.start(a_send)
    send, keep, late = normed_grad(
        here, grad_qkv, qkv_w, x_all, cols1, sums, middle_sums, ffn_sums
    )
    b_send = qkv_b.product([normed], grad_qkv, 1, 2)
    send, keep, late, b_send, qkv_b.keep, qkv_a.got, down_g.got, out_g.got = phase(
        send, keep, late, b_send, qkv_b.keep, qkv_a.got, down_g.got, out_g.got
    )
    got = swap(send, "tensor", 1)
    side = swap(late, "tensor", 1)
    qkv_b.start(b_send)
    a_send, w_send, d_send = qkv_a.split(), out_g.split(), down_g.split()
    a_send, qkv_a.keep, w_send, out_g.keep, got, keep, late, d_send, down_g.keep, up_g.got, out_other = phase(
        a_send, qkv_a.keep, w_send, out_g.keep, got, keep, late + side, d_send, down_g.keep, up_g.got,
        out_other
    )
    qkv_a.start(a_send)
    out_g.start(w_send)
    side = swap(late, "tensor", 2)
    low = low_rows(keep, got, rows)
    output = output_rows(out_keep, out_got, out_other, tokens, unit2, post_gain, post_bias, b_down)
    output, low, late, qkv_a.got, qkv_a.keep, qkv_b.got, qkv_b.keep, out_g.got = phase(
        output, low, late + side, qkv_a.got, qkv_a.keep, qkv_b.got, qkv_b.keep, out_g.got
    )
    other = swap(low, "tensor", 2)
    side = swap(late, "dp", masks[0])
    a_send, b_send = qkv_a.split(), qkv_b.split()
    a_send, qkv_a.keep, b_send, qkv_b.keep, late, d_send = phase(
        a_send, qkv_a.keep, b_send, qkv_b.keep, late + side, d_send
    )
    qkv_a.start(a_send)
    side = swap(late, "dp", masks[1])
    qkv_b.start(b_send)
    down_g.start(d_send)
    other, late, qkv_b.got, qkv_b.keep, up_g.got, out_g.got = phase(
        other, late + side, qkv_b.got, qkv_b.keep, up_g.got, out_g.got
    )
    if quick:
        b_send, late = phase(qkv_b.split(), late)
        qkv_b.start(b_send)
    input_grad = last(keep, got, other, tokens, cols1, ln1_gain, grad_hidden)
    g_up, g_out = up_g.finish(), out_g.finish()
    for mask in masks[2:]:
        late = late + swap(late, "dp", mask)
    g_down = down_g.finish()
    g_a, g_b = qkv_a.finish(), qkv_b.finish()
    extra = g_a.shape[1] - columns
    blocks = FF // D
    return (
        output,
        input_grad,
        late[0],
        late[1],
        g_a[:, :columns],
        late[2],
        jnp.concatenate([g_a[:, columns:], g_b[:, : columns - extra]], 1),
        g_b[:, columns - extra :],
        late[3],
        jnp.sum(late[4].reshape(HEADS, HD), axis=1),
        g_out,
        late[9],
        late[7],
        late[8],
        late[5],
        late[6],
        g_up,
        late[12 : 12 + blocks].reshape(FF),
        late[12 + blocks : 12 + 2 * blocks].reshape(FF),
        late[12 + 2 * blocks : 12 + 3 * blocks].reshape(FF),
        g_down,
        late[10],
    )


def solution(mesh):
    return jax.shard_map(
        per_device,
        mesh=mesh,
        in_specs=(
            P(("dp", "tensor"), None),
            P("dp", None),
            P(),
            P(),
            P("dp", "tensor"),
            P(),
            P("dp", "tensor"),
            P("dp", "tensor"),
            P(),
            P(),
            P("tensor", "dp"),
            P(),
            P(),
            P(),
            P(),
            P(),
            P("dp", "tensor"),
            P(),
            P(),
            P(),
            P("tensor", "dp"),
            P(),
            P(("dp", "tensor"), None),
        ),
        out_specs=(
            P(("dp", "tensor"), None),
            P(("dp", "tensor"), None),
            P(),
            P(),
            P("dp", "tensor"),
            P(),
            P("dp", "tensor"),
            P("dp", "tensor"),
            P(),
            P(),
            P("tensor", "dp"),
            P(),
            P(),
            P(),
            P(),
            P(),
            P("dp", "tensor"),
            P(),
            P(),
            P(),
            P("tensor", "dp"),
            P(),
        ),
        check_vma=False,
    )
```

profile of v0, /device:TPU:0, one launch (start us, length us, event | category | flops | bytes accessed | tf_op | source)
XLA Modules:
  0.0 315.6 jit_solution(7042922958793350370)
XLA Ops:
  2.4 3.0 collective-permute-start
  5.4 2.6 collective-permute-start.2
  18.7 2.2 collective-permute-done.2.refs_4_
  25.9 7.1 %norm_one.1 = (bf16[1024,1024]{1,0:T(8,128)(2,1)}, bf16[1024,1024]{1,0:T(8,128)(2,1)}, f32[1024,128]{1,0:T(8,128)}) custom-call(bf16[256,1024]{1,0:T(8,128)(2,1)} %tokens_ref.2, bf16[256,1024]{1,0:T(8,128)(2,1)} %copy-done, bf16[256,1024]{1,0:T(8,128)(2,1)} %copy-done.16, bf16[256,1024]{1,0:T(8,128)(2,1)} %copy-done.17, f32[1,1024]{1,0:T(1,128)} %bitcast.66, ...), custom_call_target="tpu_custom_call" | custom-call | tf_op jit(solution)/shard_map/norm_one/pallas_call | solution.py:386
  33.0 2.8 collective-permute-done.7.refs_6_
  38.5 2.4 collective-permute-start.13
  40.8 5.0 %collective-permute-done.11.refs_3_ = bf16[1,128,1024]{2,1,0:T(8,128)(2,1)S(1)} collective-permute-done((bf16[1,128,1024]{2,1,0:T(8,128)(2,1)}, bf16[1,128,1024]{2,1,0:T(8,128)(2,1)S(1)}, u32[]{:S(2)}, u32[]{:S(2)}) %collective-permute-start.11) | collective-permute-done | bytes 262176 | tf_op jit(solution)/shard_map/ppermute | solution.py:29
  45.8 4.7 %collective-permute-done.12.refs_7_ = bf16[1,128,1024]{2,1,0:T(8,128)(2,1)S(1)} collective-permute-done((bf16[1,128,1024]{2,1,0:T(8,128)(2,1)}, bf16[1,128,1024]{2,1,0:T(8,128)(2,1)S(1)}, u32[]{:S(2)}, u32[]{:S(2)}) %collective-permute-start.12) | collective-permute-done | bytes 262176 | tf_op jit(solution)/shard_map/ppermute | solution.py:29
  50.6 2.2 collective-permute-done.13.refs_4_
  58.5 15.9 %attend.1 = (bf16[1024,768]{1,0:T(8,128)(2,1)}, f32[1024,256]{1,0:T(8,128)}, bf16[1024,256]{1,0:T(8,128)(2,1)}, f32[4,4,256]{2,1,0:T(4,128)}, bf16[1024,768]{1,0...) custom-call(s32[4]{0:T(128)} %gather_fusion, s32[8]{0:T(128)} %iota_xor_fusion.order_ref, ...), custom_call_target="tpu_custom_call" | custom-call | tf_op jit(solution)/shard_map/attend/pallas_call | solution.py:550
  75.2 2.9 collective-permute-done.18.got_ref
  79.1 2.7 low_rows.4
  87.3 3.0 stack.1.grad_ref.refs_0_
  90.3 2.5 collective-permute-done.19.refs_3_
  92.8 4.5 %collective-permute-done.20.refs_7_ = bf16[1,128,1024]{2,1,0:T(8,128)(2,1)S(1)} collective-permute-done((bf16[1,128,1024]{2,1,0:T(8,128)(2,1)}, bf16[1,128,1024]{2,1,0:T(8,128)(2,1)S(1)}, u32[]{:S(2)}, u32[]{:S(2)}) %collective-permute-start.20) | collective-permute-done | bytes 262176 | tf_op jit(solution)/shard_map/ppermute | solution.py:29
  97.3 2.2 collective-permute-done.21.refs_4_
  103.5 3.7 %collective-permute-done.22.other_ref = bf16[512,1024]{1,0:T(8,128)(2,1)S(1)} collective-permute-done((bf16[512,1024]{1,0:T(8,128)(2,1)}, bf16[512,1024]{1,0:T(8,128)(2,1)S(1)}, u32[]{:S(2)}, u32[]{:S(2)}) %collective-permute-start.22) | collective-permute-done | bytes 1048608 | tf_op jit(solution)/shard_map/ppermute | solution.py:29
  108.2 5.2 %middle.1 = (bf16[512,1024]{1,0:T(8,128)(2,1)}, f32[512,1024]{1,0:T(8,128)}, f32[512,128]{1,0:T(8,128)}) custom-call(f32[512,1024]{1,0:T(8,128)} %get-tuple-element.331.keep_ref, bf16[512,1024]{1,0:T(8,128)(2,1)} %copy-done.9, bf16[512,1024]{1,0:T(8,128)(2,1)} %copy-done.10, bf16[256,1024]{1,0:T(8,128)(2,1)} %tokens_ref.2, bf16[256,1024]{1,0:T(8,128)(2,1)} %copy-done, ...), custom_call_target="tpu_custom_call" | custom-call | tf_op jit(solution)/shard_map/middle/pallas_call | solution.py:633
  116.2 6.9 %ffn_one.2 = (f32[512,1024]{1,0:T(8,128)}, f32[512,1024]{1,0:T(8,128)}, f32[8,512]{1,0:T(8,128)}, bf16[1024,1024]{1,0:T(8,128)(2,1)}) custom-call(s32[8]{0:T(128)} %iota_xor_fusion.order_ref, bf16[512,1024]{1,0:T(8,128)(2,1)} %get-tuple-element.339.in_ref.refs_0_, f32[1,1024]{1,0:T(1,128)} %bitcast.58, bf16[1,128,1024]{2,1,0:T(8,128)(2,1)} %bitcast.52, ...), custom_call_target="tpu_custom_call" | custom-call | tf_op jit(solution)/shard_map/ffn_one/pallas_call | solution.py:741
  124.1 7.0 %ffn_one.3 = (f32[512,1024]{1,0:T(8,128)}, f32[512,1024]{1,0:T(8,128)}, f32[8,512]{1,0:T(8,128)}, bf16[1024,1024]{1,0:T(8,128)(2,1)}) custom-call(s32[8]{0:T(128)} %iota_xor_fusion.order_ref, bf16[512,1024]{1,0:T(8,128)(2,1)} %copy-done.1, f32[1,1024]{1,0:T(1,128)} %bitcast.59, bf16[1024,1024]{1,0:T(8,128)(2,1)} %get-tuple-element.351.refs_0_.up_ref), custom_call_target="tpu_custom_call" | custom-call | tf_op jit(solution)/shard_map/ffn_one/pallas_call | solution.py:741
  132.0 10.2 %ffn_grad.1 = (f32[1024,1024]{1,0:T(8,128)}, f32[8,1024]{1,0:T(8,128)}, bf16[1024,1024]{1,0:T(8,128)(2,1)}) custom-call(s32[8]{0:T(128)} %iota_xor_fusion.order_ref, bf16[1024,1024]{1,0:T(8,128)(2,1)} %stack.1.grad_ref.refs_0_, f32[512,1024]{1,0:T(8,128)} %get-tuple-element.349.keep_ref.mk_ref, f32[512,1024]{1,0:T(8,128)} %get-tuple-element.359.send_ref.ms_ref, ...), custom_call_target="tpu_custom_call" | custom-call | tf_op jit(solution)/shard_map/ffn_grad/pallas_call | solution.py:791
  144.2 2.3 collective-permute-done.31.s2_ref
  147.6 13.0 %ffn_two.1 = (bf16[1024,1024]{1,0:T(8,128)(2,1)}, bf16[1024,1024]{1,0:T(8,128)(2,1)}, bf16[512,1024]{1,0:T(8,128)(2,1)}, f32[512,1024]{1,0:T(8,128)}, f32[8,1024]{1,0:T(8,128)}) custom-call(f32[512,1024]{1,0:T(8,128)} %get-tuple-element.349.keep_ref.mk_ref, f32[512,1024]{1,0:T(8,128)} %get-tuple-element.359.send_ref.ms_ref, ...), custom_call_target="tpu_custom_call" | custom-call | tf_op jit(solution)/shard_map/ffn_two/pallas_call | solution.py:891
  160.9 6.4 %outer.5 = (bf16[1024,512]{1,0:T(8,128)(2,1)}, f32[1024,512]{1,0:T(8,128)}) custom-call(s32[1]{0:T(128)} %bitcast.bit_ref, bf16[1024,1024]{1,0:T(8,128)(2,1)} %stack.1.grad_ref.refs_0_, bf16[1024,1024]{1,0:T(8,128)(2,1)} %get-tuple-element.394.refs_1_.inner_ref), custom_call_target="tpu_custom_call" | custom-call | tf_op jit(solution)/shard_map/outer/pallas_call | solution.py:213
  168.3 2.8 low_rows.5
  172.6 6.8 %outer.6 = (bf16[512,1024]{1,0:T(8,128)(2,1)}, f32[512,1024]{1,0:T(8,128)}) custom-call(s32[1]{0:T(128)} %bitcast.17.bit_ref, bf16[512,1024]{1,0:T(8,128)(2,1)} %get-tuple-element.339.in_ref.refs_0_, bf16[512,1024]{1,0:T(8,128)(2,1)} %copy-done.1, bf16[1024,1024]{1,0:T(8,128)(2,1)} %get-tuple-element.390.refs_2_), custom_call_target="tpu_custom_call" | custom-call | tf_op jit(solution)/shard_map/outer/pallas_call | solution.py:213
  180.9 6.0 %project.1 = (bf16[512,1024]{1,0:T(8,128)(2,1)}, f32[512,1024]{1,0:T(8,128)}) custom-call(bf16[1024,1024]{1,0:T(8,128)(2,1)} %get-tuple-element.394.refs_1_.inner_ref, bf16[1024,1024]{1,0:T(8,128)(2,1)} %get-tuple-element.395.weight_ref), custom_call_target="tpu_custom_call" | custom-call | tf_op jit(solution)/shard_map/project/pallas_call | solution.py:351
  186.9 9.8 %collective-permute-done.34.other_ref = bf16[512,1024]{1,0:T(8,128)(2,1)S(1)} collective-permute-done((bf16[512,1024]{1,0:T(8,128)(2,1)}, bf16[512,1024]{1,0:T(8,128)(2,1)S(1)}, u32[]{:S(2)}, u32[]{:S(2)}) %collective-permute-start.34) | collective-permute-done | bytes 1048608 | tf_op jit(solution)/shard_map/ppermute | solution.py:29
  198.2 2.9 split.10
  201.1 2.2 collective-permute-start.43
  203.3 7.2 %middle_back.1 = (bf16[512,1024]{1,0:T(8,128)(2,1)}, f32[256,1024]{1,0:T(8,128)}, f32[8,1024]{1,0:T(8,128)}) custom-call(f32[512,1024]{1,0:T(8,128)} %get-tuple-element.382.keep_ref, bf16[512,1024]{1,0:T(8,128)(2,1)} %copy-done.4, bf16[512,1024]{1,0:T(8,128)(2,1)} %copy-done.5, bf16[256,1024]{1,0:T(8,128)(2,1)} %mine_ref.1, bf16[256,1024]{1,0:T(8,128)(2,1)} %copy-done.3, ...), custom_call_target="tpu_custom_call" | custom-call | tf_op jit(solution)/shard_map/middle_back/pallas_call | solution.py:694
  213.6 2.8 split.11
  217.4 3.6 %outer.7 = (bf16[256,512]{1,0:T(8,128)(2,1)}, f32[256,512]{1,0:T(8,128)}) custom-call(s32[1]{0:T(128)} %bitcast.17.bit_ref, bf16[512,1024]{1,0:T(8,128)(2,1)} %get-tuple-element.426.refs_0_.own_ref, bf16[512,1024]{1,0:T(8,128)(2,1)} %copy-done.6, bf16[1024,256]{1,0:T(8,128)(2,1)} %get-tuple-element.421.refs_2_), custom_call_target="tpu_custom_call" | custom-call | tf_op jit(solution)/shard_map/outer/pallas_call | solution.py:213
  225.1 15.8 %attend_back.1 = (bf16[1024,768]{1,0:T(8,128)(2,1)}, f32[8,256]{1,0:T(8,128)}) custom-call(s32[4]{0:T(128)} %gather_fusion, bf16[1024,768]{1,0:T(8,128)(2,1)} %get-tuple-element.418.qkv_ref, bf16[512,1024]{1,0:T(8,128)(2,1)} %get-tuple-element.426.refs_0_.own_ref, bf16[512,1024]{1,0:T(8,128)(2,1)} %copy-done.6, ...), custom_call_target="tpu_custom_call" | custom-call | flops 16000000000 | tf_op jit(solution)/shard_map/attend_back/pallas_call | solution.py:580
  243.4 2.1 split.12
  245.6 4.2 %outer.8 = (bf16[512,384]{1,0:T(8,128)(2,1)}, f32[512,384]{1,0:T(8,128)}) custom-call(s32[1]{0:T(128)} %bitcast.17.bit_ref, bf16[1024,1024]{1,0:T(8,128)(2,1)} %get-tuple-element.294.normed_ref.refs_0_, bf16[1024,768]{1,0:T(8,128)(2,1)} %get-tuple-element.448.refs_1_.grad_ref), custom_call_target="tpu_custom_call" | custom-call | tf_op jit(solution)/shard_map/outer/pallas_call | solution.py:213
  250.7 4.1 %outer.9 = (bf16[512,384]{1,0:T(8,128)(2,1)}, f32[512,384]{1,0:T(8,128)}) custom-call(s32[1]{0:T(128)} %bitcast.17.bit_ref, bf16[1024,1024]{1,0:T(8,128)(2,1)} %get-tuple-element.294.normed_ref.refs_0_, bf16[1024,768]{1,0:T(8,128)(2,1)} %get-tuple-element.448.refs_1_.grad_ref), custom_call_target="tpu_custom_call" | custom-call | tf_op jit(solution)/shard_map/outer/pallas_call | solution.py:213
  256.8 6.8 %normed_grad.1 = (bf16[512,1024]{1,0:T(8,128)(2,1)}, f32[512,1024]{1,0:T(8,128)}, f32[24,1024]{1,0:T(8,128)}) custom-call(s32[1]{0:T(128)} %bitcast.18.side_ref, bf16[1024,768]{1,0:T(8,128)(2,1)} %get-tuple-element.448.refs_1_.grad_ref, bf16[1024,768]{1,0:T(8,128)(2,1)} %get-tuple-element.449.weight_ref, bf16[1024,1024]{1,0:T(8,128)(2,1)} %get-tuple-element.450.all_ref, ...), custom_call_target="tpu_custom_call" | custom-call | tf_op jit(solution)/shard_map/normed_grad/pallas_call | solution.py:958
  264.7 2.1 split.16
  268.6 2.2 split.14
  272.6 2.9 collective-permute-start.51
  275.5 2.1 low_rows.7
  277.6 2.9 output_rows.1
  281.4 2.1 split.18
  295.1 2.5 collective-permute-done.55.got_ref
  300.7 2.2 collective-permute-start.56
  305.2 3.2 %last.1 = f32[256,1024]{1,0:T(8,128)} custom-call(f32[512,1024]{1,0:T(8,128)} %get-tuple-element.480.keep_ref, bf16[512,1024]{1,0:T(8,128)(2,1)} %copy-done.8, bf16[256,1024]{1,0:T(8,128)(2,1)} %copy-done.13, bf16[256,1024]{1,0:T(8,128)(2,1)} %tokens_ref.2, f32[1024,128]{1,0:T(8,128)} %get-tuple-element.451.cols_ref, f32[1,1024]{1,0:T(1,128)} %bitcast.67, ...), custom_call_target="tpu_custom_call" | custom-call | tf_op jit(solution)/shard_map/last/pallas_call | solution.py:997
  308.4 3.2 %collective-permute-done.58 = bf16[128,384]{1,0:T(8,128)(2,1)S(1)} collective-permute-done((bf16[128,384]{1,0:T(8,128)(2,1)}, bf16[128,384]{1,0:T(8,128)(2,1)S(1)}, u32[]{:S(2)}, u32[]{:S(2)}) %collective-permute-start.58) | collective-permute-done | bytes 98336 | tf_op jit(solution)/shard_map/ppermute | solution.py:29
  (270 shorter events, 91.2 us)
Async XLA Ops:
  2.4 18.5 %collective-permute-start = (bf16[256,1024]{1,0:T(8,128)(2,1)}, bf16[256,1024]{1,0:T(8,128)(2,1)S(1)}, u32[]{:S(2)}, u32[]{:S(2)}) collective-permute-start(bf16[256,1024]{1,0:T(8,128)(2,1)} %tokens_ref.2), channel_id=1, source_target_pairs={{0,2},{1,3},{2,0},{3,1},{4,6},{5,7},{6,4},{7,5},{8,10},{9,11},{10,... | collective-permute-start | bytes 1572872 | tf_op jit(solution)/shard_map/ppermute | solution.py:29
  5.4 15.5 %collective-permute-start.1 = (bf16[256,1024]{1,0:T(8,128)(2,1)}, bf16[256,1024]{1,0:T(8,128)(2,1)S(1)}, u32[]{:S(2)}, u32[]{:S(2)}) collective-permute-start(bf16[256,1024]{1,0:T(8,128)(2,1)} %tokens_ref.2), channel_id=1, source_target_pairs={{0,1},{1,0},{2,3},{3,2},{4,5},{5,4},{6,7},{7,6},{8,9},{9,8},{10,11... | collective-permute-start | bytes 1572872 | tf_op jit(solution)/shard_map/ppermute | solution.py:29
  5.4 15.4 %collective-permute-start.2 = (bf16[1,128,1024]{2,1,0:T(8,128)(2,1)}, bf16[1,128,1024]{2,1,0:T(8,128)(2,1)S(1)}, u32[]{:S(2)}, u32[]{:S(2)}) collective-permute-start(bf16[1,128,1024]{2,1,0:T(8,128)(2,1)} %bitcast.44), channel_id=1, source_target_pairs={{0,16},{4,20},{8,24},{12,28},{16,0},{20,4},{24,8},{28,12},{1,17},{... | collective-permute-start | bytes 786440 | tf_op jit(solution)/shard_map/ppermute | solution.py:29
  8.0 12.9 %collective-permute-start.3 = (bf16[1,128,1024]{2,1,0:T(8,128)(2,1)}, bf16[1,128,1024]{2,1,0:T(8,128)(2,1)S(1)}, u32[]{:S(2)}, u32[]{:S(2)}) collective-permute-start(bf16[1,128,1024]{2,1,0:T(8,128)(2,1)} %bitcast.45), channel_id=1, source_target_pairs={{0,4},{4,0},{8,12},{12,8},{16,20},{20,16},{24,28},{28,24},{1,5},{5... | collective-permute-start | bytes 786440 | tf_op jit(solution)/shard_map/ppermute | solution.py:29
  21.0 14.8 %collective-permute-start.5 = (bf16[256,1024]{1,0:T(8,128)(2,1)}, bf16[256,1024]{1,0:T(8,128)(2,1)S(1)}, u32[]{:S(2)}, u32[]{:S(2)}) collective-permute-start(bf16[256,1024]{1,0:T(8,128)(2,1)} %mine_ref.1), channel_id=1, source_target_pairs={{0,2},{1,3},{2,0},{3,1},{4,6},{5,7},{6,4},{7,5},{8,10},{9,11},{10,... | collective-permute-start | bytes 1572872 | tf_op jit(solution)/shard_map/ppermute | solution.py:29
  21.5 11.5 %collective-permute-start.6 = (bf16[1,128,1024]{2,1,0:T(8,128)(2,1)}, bf16[1,128,1024]{2,1,0:T(8,128)(2,1)}, u32[]{:S(2)}, u32[]{:S(2)}) collective-permute-start(bf16[1,128,1024]{2,1,0:T(8,128)(2,1)} %bitcast.46), channel_id=1, source_target_pairs={{0,8},{4,12},{8,0},{12,4},{16,24},{20,28},{24,16},{28,20},{1,9},{5... | collective-permute-start | bytes 786440 | tf_op jit(solution)/shard_map/ppermute | solution.py:29
  22.4 13.5 %collective-permute-start.7 = (bf16[1,128,1024]{2,1,0:T(8,128)(2,1)S(1)}, bf16[1,128,1024]{2,1,0:T(8,128)(2,1)}, u32[]{:S(2)}, u32[]{:S(2)}) collective-permute-start(bf16[1,128,1024]{2,1,0:T(8,128)(2,1)S(1)} %collective-permute-done.2.refs_4_), channel_id=1, source_target_pairs={{0,8},{4,12},{8,0},{12,4},{16,24},{20,28},{24,16},{28,20},{1,9},{5... | collective-permute-start | bytes 786440 | tf_op jit(solution)/shard_map/ppermute | solution.py:29
  23.6 12.3 %collective-permute-start.8 = (bf16[1,128,1024]{2,1,0:T(8,128)(2,1)S(1)}, bf16[1,128,1024]{2,1,0:T(8,128)(2,1)}, u32[]{:S(2)}, u32[]{:S(2)}) collective-permute-start(bf16[1,128,1024]{2,1,0:T(8,128)(2,1)S(1)} %collective-permute-done.2.refs_4_), channel_id=1, source_target_pairs={{0,4},{4,0},{8,12},{12,8},{16,20},{20,16},{24,28},{28,24},{1,5},{5... | collective-permute-start | bytes 786440 | tf_op jit(solution)/shard_map/ppermute | solution.py:29
  35.9 16.9 %collective-permute-start.10 = (bf16[256,1024]{1,0:T(8,128)(2,1)S(1)}, bf16[256,1024]{1,0:T(8,128)(2,1)S(1)}, u32[]{:S(2)}, u32[]{:S(2)}) collective-permute-start(bf16[256,1024]{1,0:T(8,128)(2,1)S(1)} %collective-permute-done.5.refs_1_.pair_ref), channel_id=1, source_target_pairs={{0,1},{1,0},{2,3},{3,2},{4,5},{5,4},{6,7},{7,6},{8,9},{9,8},{10,11... | collective-permute-start | bytes 1572872 | tf_op jit(solution)/shard_map/ppermute | solution.py:29
  35.9 16.8 %collective-permute-start.9 = (bf16[256,1024]{1,0:T(8,128)(2,1)S(1)}, bf16[256,1024]{1,0:T(8,128)(2,1)S(1)}, u32[]{:S(2)}, u32[]{:S(2)}) collective-permute-start(bf16[256,1024]{1,0:T(8,128)(2,1)S(1)} %copy-done.2), channel_id=1, source_target_pairs={{0,1},{1,0},{2,3},{3,2},{4,5},{5,4},{6,7},{7,6},{8,9},{9,8},{10,11... | collective-permute-start | bytes 1572872 | tf_op jit(solution)/shard_map/ppermute | solution.py:29
  36.4 9.4 %collective-permute-start.11 = (bf16[1,128,1024]{2,1,0:T(8,128)(2,1)}, bf16[1,128,1024]{2,1,0:T(8,128)(2,1)S(1)}, u32[]{:S(2)}, u32[]{:S(2)}) collective-permute-start(bf16[1,128,1024]{2,1,0:T(8,128)(2,1)} %collective-permute-done.6.refs_2_), channel_id=1, source_target_pairs={{0,4},{4,0},{8,12},{12,8},{16,20},{20,16},{24,28},{28,24},{1,5},{5... | collective-permute-start | bytes 786440 | tf_op jit(solution)/shard_map/ppermute | solution.py:29
  38.0 12.6 %collective-permute-start.12 = (bf16[1,128,1024]{2,1,0:T(8,128)(2,1)}, bf16[1,128,1024]{2,1,0:T(8,128)(2,1)S(1)}, u32[]{:S(2)}, u32[]{:S(2)}) collective-permute-start(bf16[1,128,1024]{2,1,0:T(8,128)(2,1)} %collective-permute-done.7.refs_6_), channel_id=1, source_target_pairs={{0,4},{4,0},{8,12},{12,8},{16,20},{20,16},{24,28},{28,24},{1,5},{5... | collective-permute-start | bytes 786440 | tf_op jit(solution)/shard_map/ppermute | solution.py:29
  38.5 14.3 %collective-permute-start.13 = (bf16[1,128,1024]{2,1,0:T(8,128)(2,1)S(1)}, bf16[1,128,1024]{2,1,0:T(8,128)(2,1)S(1)}, u32[]{:S(2)}, u32[]{:S(2)}) collective-permute-start(bf16[1,128,1024]{2,1,0:T(8,128)(2,1)S(1)} %bitcast.53), channel_id=1, source_target_pairs={{0,16},{4,20},{8,24},{12,28},{16,0},{20,4},{24,8},{28,12},{1,17},{... | collective-permute-start | bytes 786440 | tf_op jit(solution)/shard_map/ppermute | solution.py:29
  52.7 21.7 %collective-permute-start.14 = (bf16[1,128,1024]{2,1,0:T(8,128)(2,1)S(1)}, bf16[1,128,1024]{2,1,0:T(8,128)(2,1)}, u32[]{:S(2)}, u32[]{:S(2)}) collective-permute-start(bf16[1,128,1024]{2,1,0:T(8,128)(2,1)S(1)} %bitcast.54), channel_id=1, source_target_pairs={{0,8},{4,12},{8,0},{12,4},{16,24},{20,28},{24,16},{28,20},{1,9},{5... | collective-permute-start | bytes 786440 | tf_op jit(solution)/shard_map/ppermute | solution.py:29
  53.3 21.2 %collective-permute-start.15 = (bf16[1,128,1024]{2,1,0:T(8,128)(2,1)S(1)}, bf16[1,128,1024]{2,1,0:T(8,128)(2,1)}, u32[]{:S(2)}, u32[]{:S(2)}) collective-permute-start(bf16[1,128,1024]{2,1,0:T(8,128)(2,1)S(1)} %collective-permute-done.13.refs_4_), channel_id=1, source_target_pairs={{0,8},{4,12},{8,0},{12,4},{16,24},{20,28},{24,16},{28,20},{1,9},{5... | collective-permute-start | bytes 786440 | tf_op jit(solution)/shard_map/ppermute | solution.py:29
  54.8 19.6 %collective-permute-start.16 = (bf16[1,128,1024]{2,1,0:T(8,128)(2,1)S(1)}, bf16[1,128,1024]{2,1,0:T(8,128)(2,1)S(1)}, u32[]{:S(2)}, u32[]{:S(2)}) collective-permute-start(bf16[1,128,1024]{2,1,0:T(8,128)(2,1)S(1)} %bitcast.55), channel_id=1, source_target_pairs={{0,4},{4,0},{8,12},{12,8},{16,20},{20,16},{24,28},{28,24},{1,5},{5... | collective-permute-start | bytes 786440 | tf_op jit(solution)/shard_map/ppermute | solution.py:29
  56.4 18.1 %collective-permute-start.17 = (bf16[1,128,1024]{2,1,0:T(8,128)(2,1)S(1)}, bf16[1,128,1024]{2,1,0:T(8,128)(2,1)S(1)}, u32[]{:S(2)}, u32[]{:S(2)}) collective-permute-start(bf16[1,128,1024]{2,1,0:T(8,128)(2,1)S(1)} %collective-permute-done.13.refs_4_), channel_id=1, source_target_pairs={{0,4},{4,0},{8,12},{12,8},{16,20},{20,16},{24,28},{28,24},{1,5},{5... | collective-permute-start | bytes 786440 | tf_op jit(solution)/shard_map/ppermute | solution.py:29
  81.8 25.4 %collective-permute-start.22 = (bf16[512,1024]{1,0:T(8,128)(2,1)}, bf16[512,1024]{1,0:T(8,128)(2,1)S(1)}, u32[]{:S(2)}, u32[]{:S(2)}) collective-permute-start(bf16[512,1024]{1,0:T(8,128)(2,1)} %low_rows.4), channel_id=1, source_target_pairs={{0,2},{1,3},{2,0},{3,1},{4,6},{5,7},{6,4},{7,5},{8,10},{9,11},{10,... | collective-permute-start | bytes 3145736 | tf_op jit(solution)/shard_map/ppermute | solution.py:29
  83.4 9.4 %collective-permute-start.19 = (bf16[1,128,1024]{2,1,0:T(8,128)(2,1)}, bf16[1,128,1024]{2,1,0:T(8,128)(2,1)S(1)}, u32[]{:S(2)}, u32[]{:S(2)}) collective-permute-start(bf16[1,128,1024]{2,1,0:T(8,128)(2,1)} %collective-permute-done.14.refs_2_), channel_id=1, source_target_pairs={{0,4},{4,0},{8,12},{12,8},{16,20},{20,16},{24,28},{28,24},{1,5},{5... | collective-permute-start | bytes 786440 | tf_op jit(solution)/shard_map/ppermute | solution.py:29
  84.9 12.4 %collective-permute-start.20 = (bf16[1,128,1024]{2,1,0:T(8,128)(2,1)}, bf16[1,128,1024]{2,1,0:T(8,128)(2,1)S(1)}, u32[]{:S(2)}, u32[]{:S(2)}) collective-permute-start(bf16[1,128,1024]{2,1,0:T(8,128)(2,1)} %collective-permute-done.15.refs_6_), channel_id=1, source_target_pairs={{0,4},{4,0},{8,12},{12,8},{16,20},{20,16},{24,28},{28,24},{1,5},{5... | collective-permute-start | bytes 786440 | tf_op jit(solution)/shard_map/ppermute | solution.py:29
  85.4 14.0 %collective-permute-start.21 = (bf16[1,1024,128]{2,1,0:T(8,128)(2,1)S(1)}, bf16[1,1024,128]{2,1,0:T(8,128)(2,1)S(1)}, u32[]{:S(2)}, u32[]{:S(2)}) collective-permute-start(bf16[1,1024,128]{2,1,0:T(8,128)(2,1)S(1)} %bitcast.49), channel_id=1, source_target_pairs={{0,16},{4,20},{8,24},{12,28},{16,0},{20,4},{24,8},{28,12},{1,17},{... | collective-permute-start | bytes 786440 | tf_op jit(solution)/shard_map/ppermute | solution.py:29
  99.4 14.0 %collective-permute-start.23 = (bf16[1,1024,128]{2,1,0:T(8,128)(2,1)S(1)}, bf16[1,1024,128]{2,1,0:T(8,128)(2,1)S(1)}, u32[]{:S(2)}, u32[]{:S(2)}) collective-permute-start(bf16[1,1024,128]{2,1,0:T(8,128)(2,1)S(1)} %bitcast.50), channel_id=1, source_target_pairs={{0,8},{4,12},{8,0},{12,4},{16,24},{20,28},{24,16},{28,20},{1,9},{5... | collective-permute-start | bytes 786440 | tf_op jit(solution)/shard_map/ppermute | solution.py:29
  99.4 14.0 %collective-permute-start.24 = (bf16[1,1024,128]{2,1,0:T(8,128)(2,1)S(1)}, bf16[1,1024,128]{2,1,0:T(8,128)(2,1)S(1)}, u32[]{:S(2)}, u32[]{:S(2)}) collective-permute-start(bf16[1,1024,128]{2,1,0:T(8,128)(2,1)S(1)} %collective-permute-done.21.refs_4_), channel_id=1, source_target_pairs={{0,8},{4,12},{8,0},{12,4},{16,24},{20,28},{24,16},{28,20},{1,9},{5... | collective-permute-start | bytes 786440 | tf_op jit(solution)/shard_map/ppermute | solution.py:29
  101.5 12.0 %collective-permute-start.25 = (bf16[1,1024,128]{2,1,0:T(8,128)(2,1)S(1)}, bf16[1,1024,128]{2,1,0:T(8,128)(2,1)S(1)}, u32[]{:S(2)}, u32[]{:S(2)}) collective-permute-start(bf16[1,1024,128]{2,1,0:T(8,128)(2,1)S(1)} %bitcast.51), channel_id=1, source_target_pairs={{0,4},{4,0},{8,12},{12,8},{16,20},{20,16},{24,28},{28,24},{1,5},{5... | collective-permute-start | bytes 786440 | tf_op jit(solution)/shard_map/ppermute | solution.py:29
  103.0 11.2 %collective-permute-start.26 = (bf16[1,1024,128]{2,1,0:T(8,128)(2,1)S(1)}, bf16[1,1024,128]{2,1,0:T(8,128)(2,1)S(1)}, u32[]{:S(2)}, u32[]{:S(2)}) collective-permute-start(bf16[1,1024,128]{2,1,0:T(8,128)(2,1)S(1)} %collective-permute-done.21.refs_4_), channel_id=1, source_target_pairs={{0,4},{4,0},{8,12},{12,8},{16,20},{20,16},{24,28},{28,24},{1,5},{5... | collective-permute-start | bytes 786440 | tf_op jit(solution)/shard_map/ppermute | solution.py:29
  114.2 8.9 %collective-permute-start.27 = (bf16[512,1024]{1,0:T(8,128)(2,1)}, bf16[512,1024]{1,0:T(8,128)(2,1)S(1)}, u32[]{:S(2)}, u32[]{:S(2)}) collective-permute-start(bf16[512,1024]{1,0:T(8,128)(2,1)} %get-tuple-element.339.in_ref.refs_0_), channel_id=1, source_target_pairs={{0,1},{1,0},{2,3},{3,2},{4,5},{5,4},{6,7},{7,6},{8,9},{9,8},{10,11... | collective-permute-start | bytes 3145736 | tf_op jit(solution)/shard_map/ppermute | solution.py:29
  114.2 17.0 %collective-permute-start.28 = (bf16[1,1024,128]{2,1,0:T(8,128)(2,1)S(1)}, bf16[1,1024,128]{2,1,0:T(8,128)(2,1)S(1)}, u32[]{:S(2)}, u32[]{:S(2)}) collective-permute-start(bf16[1,1024,128]{2,1,0:T(8,128)(2,1)S(1)} %collective-permute-done.23.refs_2_), channel_id=1, source_target_pairs={{0,4},{4,0},{8,12},{12,8},{16,20},{20,16},{24,28},{28,24},{1,5},{5... | collective-permute-start | bytes 786440 | tf_op jit(solution)/shard_map/ppermute | solution.py:29
  115.7 15.5 %collective-permute-start.29 = (bf16[1,1024,128]{2,1,0:T(8,128)(2,1)S(1)}, bf16[1,1024,128]{2,1,0:T(8,128)(2,1)S(1)}, u32[]{:S(2)}, u32[]{:S(2)}) collective-permute-start(bf16[1,1024,128]{2,1,0:T(8,128)(2,1)S(1)} %collective-permute-done.24.refs_6_), channel_id=1, source_target_pairs={{0,4},{4,0},{8,12},{12,8},{16,20},{20,16},{24,28},{28,24},{1,5},{5... | collective-permute-start | bytes 786440 | tf_op jit(solution)/shard_map/ppermute | solution.py:29
  171.1 25.6 %collective-permute-start.34 = (bf16[512,1024]{1,0:T(8,128)(2,1)}, bf16[512,1024]{1,0:T(8,128)(2,1)S(1)}, u32[]{:S(2)}, u32[]{:S(2)}) collective-permute-start(bf16[512,1024]{1,0:T(8,128)(2,1)} %low_rows.5), channel_id=1, source_target_pairs={{0,2},{1,3},{2,0},{3,1},{4,6},{5,7},{6,4},{7,5},{8,10},{9,11},{10,... | collective-permute-start | bytes 3145736 | tf_op jit(solution)/shard_map/ppermute | solution.py:29
  172.1 25.1 %collective-permute-start.35 = (bf16[1024,512]{1,0:T(8,128)(2,1)S(1)}, bf16[1024,512]{1,0:T(8,128)(2,1)S(1)}, u32[]{:S(2)}, u32[]{:S(2)}) collective-permute-start(bf16[1024,512]{1,0:T(8,128)(2,1)S(1)} %copy-done.45), channel_id=1, source_target_pairs={{0,8},{4,12},{8,0},{12,4},{16,24},{20,28},{24,16},{28,20},{1,9},{5... | collective-permute-start | bytes 3145736 | tf_op jit(solution)/shard_map/ppermute | solution.py:29
  179.4 31.1 %collective-permute-start.36 = (bf16[512,1024]{1,0:T(8,128)(2,1)}, bf16[512,1024]{1,0:T(8,128)(2,1)}, u32[]{:S(2)}, u32[]{:S(2)}) collective-permute-start(bf16[512,1024]{1,0:T(8,128)(2,1)} %get-tuple-element.407), channel_id=1, source_target_pairs={{0,4},{4,0},{8,12},{12,8},{16,20},{20,16},{24,28},{28,24},{1,5},{5... | collective-permute-start | bytes 3145736 | tf_op jit(solution)/shard_map/ppermute | solution.py:29
  201.1 9.4 %collective-permute-start.37 = (bf16[512,1024]{1,0:T(8,128)(2,1)}, bf16[512,1024]{1,0:T(8,128)(2,1)S(1)}, u32[]{:S(2)}, u32[]{:S(2)}) collective-permute-start(bf16[512,1024]{1,0:T(8,128)(2,1)} %get-tuple-element.408), channel_id=1, source_target_pairs={{0,1},{1,0},{2,3},{3,2},{4,5},{5,4},{6,7},{7,6},{8,9},{9,8},{10,11... | collective-permute-start | bytes 3145736 | tf_op jit(solution)/shard_map/ppermute | solution.py:29
  201.1 62.5 %collective-permute-start.43 = (bf16[1024,256]{1,0:T(8,128)(2,1)}, bf16[1024,256]{1,0:T(8,128)(2,1)S(1)}, u32[]{:S(2)}, u32[]{:S(2)}) collective-permute-start(bf16[1024,256]{1,0:T(8,128)(2,1)} %get-tuple-element.461), channel_id=1, source_target_pairs={{0,16},{4,20},{8,24},{12,28},{16,0},{20,4},{24,8},{28,12},{1,17},{... | collective-permute-start | bytes 1572872 | tf_op jit(solution)/shard_map/ppermute | solution.py:29
  221.0 19.9 %collective-permute-start.39 = (bf16[256,1024]{1,0:T(8,128)(2,1)S(1)}, bf16[256,1024]{1,0:T(8,128)(2,1)S(1)}, u32[]{:S(2)}, u32[]{:S(2)}) collective-permute-start(bf16[256,1024]{1,0:T(8,128)(2,1)S(1)} %copy-done.51), channel_id=1, source_target_pairs={{0,8},{4,12},{8,0},{12,4},{16,24},{20,28},{24,16},{28,20},{1,9},{5... | collective-permute-start | bytes 1572872 | tf_op jit(solution)/shard_map/ppermute | solution.py:29
  222.7 18.2 %collective-permute-start.40 = (bf16[256,1024]{1,0:T(8,128)(2,1)S(1)}, bf16[256,1024]{1,0:T(8,128)(2,1)S(1)}, u32[]{:S(2)}, u32[]{:S(2)}) collective-permute-start(bf16[256,1024]{1,0:T(8,128)(2,1)S(1)} %copy-done.49), channel_id=1, source_target_pairs={{0,2},{1,3},{2,0},{3,1},{4,6},{5,7},{6,4},{7,5},{8,10},{9,11},{10,... | collective-permute-start | bytes 1572872 | tf_op jit(solution)/shard_map/ppermute | solution.py:29
  223.6 17.2 %collective-permute-start.41 = (bf16[256,512]{1,0:T(8,128)(2,1)}, bf16[256,512]{1,0:T(8,128)(2,1)S(1)}, u32[]{:S(2)}, u32[]{:S(2)}) collective-permute-start(bf16[256,512]{1,0:T(8,128)(2,1)} %get-tuple-element.435), channel_id=1, source_target_pairs={{0,4},{4,0},{8,12},{12,8},{16,20},{20,16},{24,28},{28,24},{1,5},{5... | collective-permute-start | bytes 786440 | tf_op jit(solution)/shard_map/ppermute | solution.py:29
  249.8 13.8 %collective-permute-start.42 = (bf16[512,384]{1,0:T(8,128)(2,1)}, bf16[512,384]{1,0:T(8,128)(2,1)S(1)}, u32[]{:S(2)}, u32[]{:S(2)}) collective-permute-start(bf16[512,384]{1,0:T(8,128)(2,1)} %get-tuple-element.460), channel_id=1, source_target_pairs={{0,4},{4,0},{8,12},{12,8},{16,20},{20,16},{24,28},{28,24},{1,5},{5... | collective-permute-start | bytes 1179656 | tf_op jit(solution)/shard_map/ppermute | solution.py:29
  250.3 13.2 %collective-permute-start.44 = (bf16[256,256]{1,0:T(8,128)(2,1)S(1)}, bf16[256,256]{1,0:T(8,128)(2,1)S(1)}, u32[]{:S(2)}, u32[]{:S(2)}) collective-permute-start(bf16[256,256]{1,0:T(8,128)(2,1)S(1)} %copy-done.61), channel_id=1, source_target_pairs={{0,8},{4,12},{8,0},{12,4},{16,24},{20,28},{24,16},{28,20},{1,9},{5... | collective-permute-start | bytes 393224 | tf_op jit(solution)/shard_map/ppermute | solution.py:29
  254.8 15.9 %collective-permute-start.47 = (bf16[128,1024]{1,0:T(8,128)(2,1)}, bf16[128,1024]{1,0:T(8,128)(2,1)S(1)}, u32[]{:S(2)}, u32[]{:S(2)}) collective-permute-start(bf16[128,1024]{1,0:T(8,128)(2,1)} %get-tuple-element.477), channel_id=1, source_target_pairs={{0,16},{4,20},{8,24},{12,28},{16,0},{20,4},{24,8},{28,12},{1,17},{... | collective-permute-start | bytes 786440 | tf_op jit(solution)/shard_map/ppermute | solution.py:29
  263.6 7.1 %collective-permute-start.46 = (f32[24,1024]{1,0:T(8,128)}, f32[24,1024]{1,0:T(8,128)S(1)}, u32[]{:S(2)}, u32[]{:S(2)}) collective-permute-start(f32[24,1024]{1,0:T(8,128)} %get-tuple-element.472), channel_id=1, source_target_pairs={{0,1},{1,0},{2,3},{3,2},{4,5},{5,4},{6,7},{7,6},{8,9},{9,8},{10,11... | collective-permute-start | bytes 294920 | tf_op jit(solution)/shard_map/ppermute | solution.py:29
  263.7 7.1 %collective-permute-start.45 = (bf16[512,1024]{1,0:T(8,128)(2,1)}, bf16[512,1024]{1,0:T(8,128)(2,1)S(1)}, u32[]{:S(2)}, u32[]{:S(2)}) collective-permute-start(bf16[512,1024]{1,0:T(8,128)(2,1)} %get-tuple-element.470), channel_id=1, source_target_pairs={{0,1},{1,0},{2,3},{3,2},{4,5},{5,4},{6,7},{7,6},{8,9},{9,8},{10,11... | collective-permute-start | bytes 3145736 | tf_op jit(solution)/shard_map/ppermute | solution.py:29
  264.2 16.4 %collective-permute-start.50 = (bf16[512,384]{1,0:T(8,128)(2,1)S(1)}, bf16[512,384]{1,0:T(8,128)(2,1)S(1)}, u32[]{:S(2)}, u32[]{:S(2)}) collective-permute-start(bf16[512,384]{1,0:T(8,128)(2,1)S(1)} %copy-done.52), channel_id=1, source_target_pairs={{0,4},{4,0},{8,12},{12,8},{16,20},{20,16},{24,28},{28,24},{1,5},{5... | collective-permute-start | bytes 1179656 | tf_op jit(solution)/shard_map/ppermute | solution.py:29
  270.8 9.8 %collective-permute-start.48 = (f32[24,1024]{1,0:T(8,128)S(1)}, f32[24,1024]{1,0:T(8,128)S(1)}, u32[]{:S(2)}, u32[]{:S(2)}) collective-permute-start(f32[24,1024]{1,0:T(8,128)S(1)} %add.84), channel_id=1, source_target_pairs={{0,2},{1,3},{2,0},{3,1},{4,6},{5,7},{6,4},{7,5},{8,10},{9,11},{10,... | collective-permute-start | bytes 294920 | tf_op jit(solution)/shard_map/ppermute | solution.py:29
  271.9 8.7 %collective-permute-start.49 = (bf16[256,384]{1,0:T(8,128)(2,1)}, bf16[256,384]{1,0:T(8,128)(2,1)S(1)}, u32[]{:S(2)}, u32[]{:S(2)}) collective-permute-start(bf16[256,384]{1,0:T(8,128)(2,1)} %get-tuple-element.483), channel_id=1, source_target_pairs={{0,8},{4,12},{8,0},{12,4},{16,24},{20,28},{24,16},{28,20},{1,9},{5... | collective-permute-start | bytes 589832 | tf_op jit(solution)/shard_map/ppermute | solution.py:29
  272.6 8.0 %collective-permute-start.51 = (bf16[256,128]{1,0:T(8,128)(2,1)S(1)}, bf16[256,128]{1,0:T(8,128)(2,1)S(1)}, u32[]{:S(2)}, u32[]{:S(2)}) collective-permute-start(bf16[256,128]{1,0:T(8,128)(2,1)S(1)} %copy-done.62), channel_id=1, source_target_pairs={{0,16},{4,20},{8,24},{12,28},{16,0},{20,4},{24,8},{28,12},{1,17},{... | collective-permute-start | bytes 196616 | tf_op jit(solution)/shard_map/ppermute | solution.py:29
  286.6 12.1 %collective-permute-start.52 = (bf16[256,1024]{1,0:T(8,128)(2,1)S(1)}, bf16[256,1024]{1,0:T(8,128)(2,1)S(1)}, u32[]{:S(2)}, u32[]{:S(2)}) collective-permute-start(bf16[256,1024]{1,0:T(8,128)(2,1)S(1)} %copy-done.48), channel_id=1, source_target_pairs={{0,2},{1,3},{2,0},{3,1},{4,6},{5,7},{6,4},{7,5},{8,10},{9,11},{10,... | collective-permute-start | bytes 1572872 | tf_op jit(solution)/shard_map/ppermute | solution.py:29
  300.7 11.6 %collective-permute-start.56 = (f32[24,1024]{1,0:T(8,128)S(1)}, f32[24,1024]{1,0:T(8,128)S(1)}, u32[]{:S(2)}, u32[]{:S(2)}) collective-permute-start(f32[24,1024]{1,0:T(8,128)S(1)} %add.87), channel_id=1, source_target_pairs={{0,16},{4,20},{8,24},{12,28},{16,0},{20,4},{24,8},{28,12},{1,17},{... | collective-permute-start | bytes 294920 | tf_op jit(solution)/shard_map/ppermute | solution.py:29
  303.0 8.6 %collective-permute-start.58 = (bf16[128,384]{1,0:T(8,128)(2,1)}, bf16[128,384]{1,0:T(8,128)(2,1)S(1)}, u32[]{:S(2)}, u32[]{:S(2)}) collective-permute-start(bf16[128,384]{1,0:T(8,128)(2,1)} %get-tuple-element.515), channel_id=1, source_target_pairs={{0,16},{4,20},{8,24},{12,28},{16,0},{20,4},{24,8},{28,12},{1,17},{... | collective-permute-start | bytes 294920 | tf_op jit(solution)/shard_map/ppermute | solution.py:29
  (76 other events, 642.9 us)
where the time goes:
time: 317 us; the launch traced here: 316 us
  Pallas kernels  168 us (53%)
  starting transfers between devices  61 us (19%)
  waiting for transfers between devices  55.4 us (17%)
  local copies, waits for them, and re-layouts  24.1 us (8%)
  other arithmetic  5.21 us (2%)
    ppermute x60, starting transfers between devices, swap(): return lax.ppermute(value, axis, [(i, i ^ mask) for i in range(size)])  61 us
    ppermute x60, waiting for transfers between devices, swap(): return lax.ppermute(value, axis, [(i, i ^ mask) for i in range(size)])  55.4 us
    pallas_call x5, Pallas kernels, outer(): pl.pallas_call(functools.partial(outer_kernel, width, on_left, len(picked...  25.1 us
    pallas_call x10, Pallas kernels, split(): pl.pallas_call(functools.partial(split_kernel, axis, width), grid=(size /...  21.6 us
    pallas_call x1, Pallas kernels, attend(): pl.pallas_call(functools.partial(attend_kernel, size, masks), out_shape=(...  15.9 us
    pallas_call x1, Pallas kernels, attend_back(): pl.pallas_call(functools.partial(attend_back_kernel, size), out_shape=(sh...  15.8 us
    pallas_call x2, Pallas kernels, ffn_one(): pl.pallas_call(functools.partial(ffn_one_kernel, masks), grid=(rows // si...  13.9 us
    pallas_call x1, Pallas kernels, ffn_two(): pl.pallas_call(ffn_two_kernel, grid=(2 * half,), out_shape=(shaped((2 * r...  13 us
  transfers between devices with their start and end apart: 60, of which 20 were waited for; matrix products, arithmetic and copies ran while one was open for 5% of the time, Pallas kernels for 43%

commit v1 on v0

--- a/solution.py
+++ b/solution.py
@@ -1119,17 +1119,19 @@
         up_s.put([0], [own_up])
         up_s.send(4, 0)
         attn_masks, attn_full = attn.all()
-        first = up_s.get(4)
+        far = up_s.get(4)
+    else:
+        far = []
     g_side = swap(cotangent, "tensor", 1)
     g_cross = swap(g_pair, "tensor", 1)
-    (normed, own_down, own_up, g_side, g_cross), attn_full, first = phase(
-        (normed, own_down, own_up, g_side, g_cross), attn_full, first)
+    (normed, own_down, own_up, g_side, g_cross), attn_full = phase(
+        (normed, own_down, own_up, g_side, g_cross), attn_full)
 
     if quick:
-        up_s.put([0, 4], [own_up] + first)
-        up_s.send(2, 0, 4)
-        up_s.send(1, 0, 4)
-        first = up_s.get(2, 6, 1, 5)
+        up_s.put([0], [own_up])
+        up_s.send(2, 0)
+        up_s.send(1, 0)
+        first = far + up_s.get(2, 1)
     qkv, mixed, scaled, lse, qkv_w, out_w, send, keep = attend(
         place, order_dp, normed, attn_masks, attn_full, row(qkv_b), seg_col, seg_row, scale_row
     )
@@ -1138,22 +1140,24 @@
 
     got = swap(send, "tensor", 1)
     if quick:
-        up_s.put([2, 6, 1, 5], first)
-        up_s.send(1, 2, 6)
+        up_s.put([4, 2, 1], first)
+        up_s.send(2, 4)
+        up_s.send(1, 4, 2)
         down_s.put([0], [own_down])
         down_s.send(4, 0)
-        first = up_s.get(3, 7) + down_s.get(4)
+        down_s.send(1, 0)
+        first = up_s.get(6, 5, 3) + down_s.get(4, 1)
     low, got, keep, g_side = phase(low_rows(keep, got, two), got, keep, g_side)
     other = swap(low, "tensor", 2)
     (g_all, own_down), first = phase((stack(cotangent, g_pair, g_side, g_cross), own_down), first)
     if quick:
-        up_s.put([3, 7], first[:2])
-        down_s.put([0, 4], [own_down, first[2]])
+        up_s.put([6, 5, 3], first[:3])
+        down_s.put([0, 4, 1], [own_down] + first[3:])
+        up_s.send(1, 6)
         down_s.send(2, 0, 4)
-        down_s.send(1, 0, 4)
+        down_s.send(1, 4)
         other, keep, got = phase(other, keep, got)
-        up_masks, up_full = up_s.all()
-        first = down_s.get(2, 6, 1, 5)
+        first = down_s.get(2, 6, 5) + up_s.get(7)
 
     ffn_in, unit2, cols = middle(
         keep, got, other, tokens, x_pair, b_out, post_gain, post_bias, ln2_gain, ln2_bias
@@ -1161,7 +1165,9 @@
     (ffn_in, unit2, cols), first = phase((ffn_in, unit2, cols), first)
     ffn_rest = swap(ffn_in, "tensor", 1)
     if quick:
-        down_s.put([2, 6, 1, 5], first)
+        down_s.put([2, 6, 5], first[:3])
+        up_s.put([7], first[3:])
+        up_masks, up_full = up_s.all()
         down_s.send(1, 2, 6)
         down_masks, down_full = down_s.all()
     active_k, slope_k, stats_k, up_w = ffn_one(ffn_in, order_dp, up_masks, up_full, b_up_here)
@@ -1265,11 +1271,11 @@
     side = swap(late, "dp", masks[1])
     qkv_b.start(b_send)
     down_g.start(d_send)
-    other, late, qkv_b.got, qkv_b.keep, up_g.got, out_g.got = phase(
-        other, late + side, qkv_b.got, qkv_b.keep, up_g.got, out_g.got
+    late, qkv_b.got, qkv_b.keep, up_g.got, out_g.got = phase(
+        late + side, qkv_b.got, qkv_b.keep, up_g.got, out_g.got
     )
     if quick:
-        b_send, late = phase(qkv_b.split(), late)
+        b_send, late, other = phase(qkv_b.split(), late, other)
         qkv_b.start(b_send)
     input_grad = last(keep, got, other, tokens, cols1, ln1_gain, grad_hidden)
     g_up, g_out = up_g.finish(), out_g.finish()

time: 317 us -> 315 us (level)
  waiting for transfers between devices: 55.4 us -> 52 us
    ppermute x60, waiting for transfers between devices: 55.4 us -> 52 us  [swap(): return lax.ppermute(value, axis, [(i, i ^ mask) for i in range(size)])]
  transfers between devices with their start and end apart: 60 -> 60, of which waited for: 20 -> 18; matrix products, arithmetic and copies ran while one was open for 5% -> 5% of each run, Pallas kernels for 43% -> 44%
where the time goes in v1:
time: 315 us; the launch traced here: 313 us
  Pallas kernels  168 us (53%)
  starting transfers between devices  62.1 us (20%)
  waiting for transfers between devices  52 us (17%)
  local copies, waits for them, and re-layouts  24.3 us (8%)
  other arithmetic  5.21 us (2%)
    ppermute x60, starting transfers between devices, swap(): return lax.ppermute(value, axis, [(i, i ^ mask) for i in range(size)])  62.1 us
    ppermute x60, waiting for transfers between devices, swap(): return lax.ppermute(value, axis, [(i, i ^ mask) for i in range(size)])  52 us
    pallas_call x5, Pallas kernels, outer(): pl.pallas_call(functools.partial(outer_kernel, width, on_left, len(picked...  25.1 us
    pallas_call x10, Pallas kernels, split(): pl.pallas_call(functools.partial(split_kernel, axis, width), grid=(size /...  21.4 us
    pallas_call x1, Pallas kernels, attend(): pl.pallas_call(functools.partial(attend_kernel, size, masks), out_shape=(...  15.9 us
    pallas_call x1, Pallas kernels, attend_back(): pl.pallas_call(functools.partial(attend_back_kernel, size), out_shape=(sh...  15.8 us
    pallas_call x2, Pallas kernels, ffn_one(): pl.pallas_call(functools.partial(ffn_one_kernel, masks), grid=(rows // si...  13.9 us
    pallas_call x1, Pallas kernels, ffn_two(): pl.pallas_call(ffn_two_kernel, grid=(2 * half,), out_shape=(shaped((2 * r...  13 us
  transfers between devices with their start and end apart: 60, of which 18 were waited for; matrix products, arithmetic and copies ran while one was open for 5% of the time, Pallas kernels for 44%

profile of v1, /device:TPU:0, one launch (start us, length us, event | category | flops | bytes accessed | tf_op | source)
XLA Modules:
  0.0 313.2 jit_solution(11888024207544493535)
XLA Ops:
  2.4 3.0 collective-permute-start
  5.4 2.6 collective-permute-start.2
  18.7 2.2 collective-permute-done.2.refs_4_
  25.9 7.1 %norm_one.1 = (bf16[1024,1024]{1,0:T(8,128)(2,1)}, bf16[1024,1024]{1,0:T(8,128)(2,1)}, f32[1024,128]{1,0:T(8,128)}) custom-call(bf16[256,1024]{1,0:T(8,128)(2,1)} %tokens_ref.2, bf16[256,1024]{1,0:T(8,128)(2,1)} %copy-done, bf16[256,1024]{1,0:T(8,128)(2,1)} %copy-done.16, bf16[256,1024]{1,0:T(8,128)(2,1)} %copy-done.17, f32[1,1024]{1,0:T(1,128)} %bitcast.66, ...), custom_call_target="tpu_custom_call" | custom-call | tf_op jit(solution)/shard_map/norm_one/pallas_call | solution.py:386
  33.0 2.8 collective-permute-done.7.refs_6_
  38.5 2.4 collective-permute-start.13
  40.8 5.0 %collective-permute-done.11.refs_3_ = bf16[1,128,1024]{2,1,0:T(8,128)(2,1)S(1)} collective-permute-done((bf16[1,128,1024]{2,1,0:T(8,128)(2,1)}, bf16[1,128,1024]{2,1,0:T(8,128)(2,1)S(1)}, u32[]{:S(2)}, u32[]{:S(2)}) %collective-permute-start.11) | collective-permute-done | bytes 262176 | tf_op jit(solution)/shard_map/ppermute | solution.py:29
  45.8 4.7 %collective-permute-done.12.refs_7_ = bf16[1,128,1024]{2,1,0:T(8,128)(2,1)S(1)} collective-permute-done((bf16[1,128,1024]{2,1,0:T(8,128)(2,1)}, bf16[1,128,1024]{2,1,0:T(8,128)(2,1)S(1)}, u32[]{:S(2)}, u32[]{:S(2)}) %collective-permute-start.12) | collective-permute-done | bytes 262176 | tf_op jit(solution)/shard_map/ppermute | solution.py:29
  54.6 15.9 %attend.1 = (bf16[1024,768]{1,0:T(8,128)(2,1)}, f32[1024,256]{1,0:T(8,128)}, bf16[1024,256]{1,0:T(8,128)(2,1)}, f32[4,4,256]{2,1,0:T(4,128)}, bf16[1024,768]{1,0...) custom-call(s32[4]{0:T(128)} %gather_fusion, s32[8]{0:T(128)} %iota_xor_fusion.order_ref, ...), custom_call_target="tpu_custom_call" | custom-call | tf_op jit(solution)/shard_map/attend/pallas_call | solution.py:550
  71.3 2.9 collective-permute-done.16.got_ref
  75.2 2.7 low_rows.4
  82.7 2.3 collective-permute-start.20
  85.0 7.5 %collective-permute-done.17.refs_6_ = bf16[1,128,1024]{2,1,0:T(8,128)(2,1)S(1)} collective-permute-done((bf16[1,128,1024]{2,1,0:T(8,128)(2,1)S(1)}, bf16[1,128,1024]{2,1,0:T(8,128)(2,1)S(1)}, u32[]{:S(2)}, u32[]{:S(2)}) %collective-permute-start.17) | collective-permute-done | bytes 262176 | tf_op jit(solution)/shard_map/ppermute | solution.py:29
  93.1 3.0 stack.1.grad_ref.refs_0_
  96.8 2.9 collective-permute-done.21.refs_1_
  104.7 5.2 %middle.1 = (bf16[512,1024]{1,0:T(8,128)(2,1)}, f32[512,1024]{1,0:T(8,128)}, f32[512,128]{1,0:T(8,128)}) custom-call(f32[512,1024]{1,0:T(8,128)} %get-tuple-element.330.keep_ref, bf16[512,1024]{1,0:T(8,128)(2,1)} %copy-done.9, bf16[512,1024]{1,0:T(8,128)(2,1)} %copy-done.10, bf16[256,1024]{1,0:T(8,128)(2,1)} %tokens_ref.2, bf16[256,1024]{1,0:T(8,128)(2,1)} %copy-done, ...), custom_call_target="tpu_custom_call" | custom-call | tf_op jit(solution)/shard_map/middle/pallas_call | solution.py:633
  115.1 6.9 %ffn_one.2 = (f32[512,1024]{1,0:T(8,128)}, f32[512,1024]{1,0:T(8,128)}, f32[8,512]{1,0:T(8,128)}, bf16[1024,1024]{1,0:T(8,128)(2,1)}) custom-call(s32[8]{0:T(128)} %iota_xor_fusion.order_ref, bf16[512,1024]{1,0:T(8,128)(2,1)} %get-tuple-element.339.in_ref.refs_0_, f32[1,1024]{1,0:T(1,128)} %bitcast.58, bf16[1,128,1024]{2,1,0:T(8,128)(2,1)} %bitcast.52, ...), custom_call_target="tpu_custom_call" | custom-call | tf_op jit(solution)/shard_map/ffn_one/pallas_call | solution.py:741
  123.0 7.0 %ffn_one.3 = (f32[512,1024]{1,0:T(8,128)}, f32[512,1024]{1,0:T(8,128)}, f32[8,512]{1,0:T(8,128)}, bf16[1024,1024]{1,0:T(8,128)(2,1)}) custom-call(s32[8]{0:T(128)} %iota_xor_fusion.order_ref, bf16[512,1024]{1,0:T(8,128)(2,1)} %copy-done.1, f32[1,1024]{1,0:T(1,128)} %bitcast.59, bf16[1024,1024]{1,0:T(8,128)(2,1)} %get-tuple-element.351.refs_0_.up_ref), custom_call_target="tpu_custom_call" | custom-call | tf_op jit(solution)/shard_map/ffn_one/pallas_call | solution.py:741
  130.8 10.2 %ffn_grad.1 = (f32[1024,1024]{1,0:T(8,128)}, f32[8,1024]{1,0:T(8,128)}, bf16[1024,1024]{1,0:T(8,128)(2,1)}) custom-call(s32[8]{0:T(128)} %iota_xor_fusion.order_ref, bf16[1024,1024]{1,0:T(8,128)(2,1)} %stack.1.grad_ref.refs_0_, f32[512,1024]{1,0:T(8,128)} %get-tuple-element.349.keep_ref.mk_ref, f32[512,1024]{1,0:T(8,128)} %get-tuple-element.359.send_ref.ms_ref, ...), custom_call_target="tpu_custom_call" | custom-call | tf_op jit(solution)/shard_map/ffn_grad/pallas_call | solution.py:791
  143.0 2.6 collective-permute-done.31.s2_ref
  146.3 13.0 %ffn_two.1 = (bf16[1024,1024]{1,0:T(8,128)(2,1)}, bf16[1024,1024]{1,0:T(8,128)(2,1)}, bf16[512,1024]{1,0:T(8,128)(2,1)}, f32[512,1024]{1,0:T(8,128)}, f32[8,1024]{1,0:T(8,128)}) custom-call(f32[512,1024]{1,0:T(8,128)} %get-tuple-element.349.keep_ref.mk_ref, f32[512,1024]{1,0:T(8,128)} %get-tuple-element.359.send_ref.ms_ref, ...), custom_call_target="tpu_custom_call" | custom-call | tf_op jit(solution)/shard_map/ffn_two/pallas_call | solution.py:891
  159.6 6.4 %outer.5 = (bf16[1024,512]{1,0:T(8,128)(2,1)}, f32[1024,512]{1,0:T(8,128)}) custom-call(s32[1]{0:T(128)} %bitcast.bit_ref, bf16[1024,1024]{1,0:T(8,128)(2,1)} %stack.1.grad_ref.refs_0_, bf16[1024,1024]{1,0:T(8,128)(2,1)} %get-tuple-element.394.refs_1_.inner_ref), custom_call_target="tpu_custom_call" | custom-call | tf_op jit(solution)/shard_map/outer/pallas_call | solution.py:213
  167.0 2.8 low_rows.5
  172.4 6.8 %outer.6 = (bf16[512,1024]{1,0:T(8,128)(2,1)}, f32[512,1024]{1,0:T(8,128)}) custom-call(s32[1]{0:T(128)} %bitcast.17.bit_ref, bf16[512,1024]{1,0:T(8,128)(2,1)} %get-tuple-element.339.in_ref.refs_0_, bf16[512,1024]{1,0:T(8,128)(2,1)} %copy-done.1, bf16[1024,1024]{1,0:T(8,128)(2,1)} %get-tuple-element.390.refs_2_), custom_call_target="tpu_custom_call" | custom-call | tf_op jit(solution)/shard_map/outer/pallas_call | solution.py:213
  179.7 6.0 %project.1 = (bf16[512,1024]{1,0:T(8,128)(2,1)}, f32[512,1024]{1,0:T(8,128)}) custom-call(bf16[1024,1024]{1,0:T(8,128)(2,1)} %get-tuple-element.394.refs_1_.inner_ref, bf16[1024,1024]{1,0:T(8,128)(2,1)} %get-tuple-element.395.weight_ref), custom_call_target="tpu_custom_call" | custom-call | tf_op jit(solution)/shard_map/project/pallas_call | solution.py:351
  185.7 9.7 %collective-permute-done.34.other_ref = bf16[512,1024]{1,0:T(8,128)(2,1)S(1)} collective-permute-done((bf16[512,1024]{1,0:T(8,128)(2,1)}, bf16[512,1024]{1,0:T(8,128)(2,1)S(1)}, u32[]{:S(2)}, u32[]{:S(2)}) %collective-permute-start.34) | collective-permute-done | bytes 1048608 | tf_op jit(solution)/shard_map/ppermute | solution.py:29
  197.1 2.9 split.10
  199.9 3.1 collective-permute-start.43
  203.0 7.2 %middle_back.1 = (bf16[512,1024]{1,0:T(8,128)(2,1)}, f32[256,1024]{1,0:T(8,128)}, f32[8,1024]{1,0:T(8,128)}) custom-call(f32[512,1024]{1,0:T(8,128)} %get-tuple-element.382.keep_ref, bf16[512,1024]{1,0:T(8,128)(2,1)} %copy-done.4, bf16[512,1024]{1,0:T(8,128)(2,1)} %copy-done.5, bf16[256,1024]{1,0:T(8,128)(2,1)} %mine_ref.1, bf16[256,1024]{1,0:T(8,128)(2,1)} %copy-done.3, ...), custom_call_target="tpu_custom_call" | custom-call | tf_op jit(solution)/shard_map/middle_back/pallas_call | solution.py:694
  211.2 2.1 low_rows.6
  213.3 2.8 split.11
  217.1 3.6 %outer.7 = (bf16[256,512]{1,0:T(8,128)(2,1)}, f32[256,512]{1,0:T(8,128)}) custom-call(s32[1]{0:T(128)} %bitcast.17.bit_ref, bf16[512,1024]{1,0:T(8,128)(2,1)} %get-tuple-element.426.refs_0_.own_ref, bf16[512,1024]{1,0:T(8,128)(2,1)} %copy-done.6, bf16[1024,256]{1,0:T(8,128)(2,1)} %get-tuple-element.421.refs_2_), custom_call_target="tpu_custom_call" | custom-call | tf_op jit(solution)/shard_map/outer/pallas_call | solution.py:213
  223.8 15.8 %attend_back.1 = (bf16[1024,768]{1,0:T(8,128)(2,1)}, f32[8,256]{1,0:T(8,128)}) custom-call(s32[4]{0:T(128)} %gather_fusion, bf16[1024,768]{1,0:T(8,128)(2,1)} %get-tuple-element.418.qkv_ref, bf16[512,1024]{1,0:T(8,128)(2,1)} %get-tuple-element.426.refs_0_.own_ref, bf16[512,1024]{1,0:T(8,128)(2,1)} %copy-done.6, ...), custom_call_target="tpu_custom_call" | custom-call | flops 16000000000 | tf_op jit(solution)/shard_map/attend_back/pallas_call | solution.py:580
  240.2 1.8 split.13
  242.1 2.1 split.12
  244.2 4.2 %outer.8 = (bf16[512,384]{1,0:T(8,128)(2,1)}, f32[512,384]{1,0:T(8,128)}) custom-call(s32[1]{0:T(128)} %bitcast.17.bit_ref, bf16[1024,1024]{1,0:T(8,128)(2,1)} %get-tuple-element.294.normed_ref.refs_0_, bf16[1024,768]{1,0:T(8,128)(2,1)} %get-tuple-element.448.refs_1_.grad_ref), custom_call_target="tpu_custom_call" | custom-call | tf_op jit(solution)/shard_map/outer/pallas_call | solution.py:213
  250.2 4.1 %outer.9 = (bf16[512,384]{1,0:T(8,128)(2,1)}, f32[512,384]{1,0:T(8,128)}) custom-call(s32[1]{0:T(128)} %bitcast.17.bit_ref, bf16[1024,1024]{1,0:T(8,128)(2,1)} %get-tuple-element.294.normed_ref.refs_0_, bf16[1024,768]{1,0:T(8,128)(2,1)} %get-tuple-element.448.refs_1_.grad_ref), custom_call_target="tpu_custom_call" | custom-call | tf_op jit(solution)/shard_map/outer/pallas_call | solution.py:213
  255.6 6.8 %normed_grad.1 = (bf16[512,1024]{1,0:T(8,128)(2,1)}, f32[512,1024]{1,0:T(8,128)}, f32[24,1024]{1,0:T(8,128)}) custom-call(s32[1]{0:T(128)} %bitcast.18.side_ref, bf16[1024,768]{1,0:T(8,128)(2,1)} %get-tuple-element.448.refs_1_.grad_ref, bf16[1024,768]{1,0:T(8,128)(2,1)} %get-tuple-element.449.weight_ref, bf16[1024,1024]{1,0:T(8,128)(2,1)} %get-tuple-element.450.all_ref, ...), custom_call_target="tpu_custom_call" | custom-call | tf_op jit(solution)/shard_map/normed_grad/pallas_call | solution.py:958
  264.5 2.1 split.16
  268.3 2.2 split.14
  271.4 2.8 collective-permute-start.51
  274.3 2.1 low_rows.7
  276.4 2.9 output_rows.1
  280.9 2.1 split.18
  283.0 1.9 split.17
  293.5 3.0 collective-permute-done.54.got_ref
  303.7 3.2 %last.1 = f32[256,1024]{1,0:T(8,128)} custom-call(f32[512,1024]{1,0:T(8,128)} %get-tuple-element.480.keep_ref, bf16[512,1024]{1,0:T(8,128)(2,1)} %copy-done.8, bf16[256,1024]{1,0:T(8,128)(2,1)} %copy-done.13, bf16[256,1024]{1,0:T(8,128)(2,1)} %tokens_ref.2, f32[1024,128]{1,0:T(8,128)} %get-tuple-element.451.cols_ref, f32[1,1024]{1,0:T(1,128)} %bitcast.67, ...), custom_call_target="tpu_custom_call" | custom-call | tf_op jit(solution)/shard_map/last/pallas_call | solution.py:997
  306.9 2.1 collective-permute-done.58
  (270 shorter events, 87.3 us)
Async XLA Ops:
  2.4 18.5 %collective-permute-start = (bf16[256,1024]{1,0:T(8,128)(2,1)}, bf16[256,1024]{1,0:T(8,128)(2,1)S(1)}, u32[]{:S(2)}, u32[]{:S(2)}) collective-permute-start(bf16[256,1024]{1,0:T(8,128)(2,1)} %tokens_ref.2), channel_id=1, source_target_pairs={{0,2},{1,3},{2,0},{3,1},{4,6},{5,7},{6,4},{7,5},{8,10},{9,11},{10,... | collective-permute-start | bytes 1572872 | tf_op jit(solution)/shard_map/ppermute | solution.py:29
  5.4 15.5 %collective-permute-start.1 = (bf16[256,1024]{1,0:T(8,128)(2,1)}, bf16[256,1024]{1,0:T(8,128)(2,1)S(1)}, u32[]{:S(2)}, u32[]{:S(2)}) collective-permute-start(bf16[256,1024]{1,0:T(8,128)(2,1)} %tokens_ref.2), channel_id=1, source_target_pairs={{0,1},{1,0},{2,3},{3,2},{4,5},{5,4},{6,7},{7,6},{8,9},{9,8},{10,11... | collective-permute-start | bytes 1572872 | tf_op jit(solution)/shard_map/ppermute | solution.py:29
  5.4 15.4 %collective-permute-start.2 = (bf16[1,128,1024]{2,1,0:T(8,128)(2,1)}, bf16[1,128,1024]{2,1,0:T(8,128)(2,1)S(1)}, u32[]{:S(2)}, u32[]{:S(2)}) collective-permute-start(bf16[1,128,1024]{2,1,0:T(8,128)(2,1)} %bitcast.44), channel_id=1, source_target_pairs={{0,16},{4,20},{8,24},{12,28},{16,0},{20,4},{24,8},{28,12},{1,17},{... | collective-permute-start | bytes 786440 | tf_op jit(solution)/shard_map/ppermute | solution.py:29
  8.0 12.9 %collective-permute-start.3 = (bf16[1,128,1024]{2,1,0:T(8,128)(2,1)}, bf16[1,128,1024]{2,1,0:T(8,128)(2,1)S(1)}, u32[]{:S(2)}, u32[]{:S(2)}) collective-permute-start(bf16[1,128,1024]{2,1,0:T(8,128)(2,1)} %bitcast.45), channel_id=1, source_target_pairs={{0,4},{4,0},{8,12},{12,8},{16,20},{20,16},{24,28},{28,24},{1,5},{5... | collective-permute-start | bytes 786440 | tf_op jit(solution)/shard_map/ppermute | solution.py:29
  21.0 14.8 %collective-permute-start.5 = (bf16[256,1024]{1,0:T(8,128)(2,1)}, bf16[256,1024]{1,0:T(8,128)(2,1)S(1)}, u32[]{:S(2)}, u32[]{:S(2)}) collective-permute-start(bf16[256,1024]{1,0:T(8,128)(2,1)} %mine_ref.1), channel_id=1, source_target_pairs={{0,2},{1,3},{2,0},{3,1},{4,6},{5,7},{6,4},{7,5},{8,10},{9,11},{10,... | collective-permute-start | bytes 1572872 | tf_op jit(solution)/shard_map/ppermute | solution.py:29
  21.5 11.5 %collective-permute-start.6 = (bf16[1,128,1024]{2,1,0:T(8,128)(2,1)}, bf16[1,128,1024]{2,1,0:T(8,128)(2,1)}, u32[]{:S(2)}, u32[]{:S(2)}) collective-permute-start(bf16[1,128,1024]{2,1,0:T(8,128)(2,1)} %bitcast.46), channel_id=1, source_target_pairs={{0,8},{4,12},{8,0},{12,4},{16,24},{20,28},{24,16},{28,20},{1,9},{5... | collective-permute-start | bytes 786440 | tf_op jit(solution)/shard_map/ppermute | solution.py:29
  22.4 13.5 %collective-permute-start.7 = (bf16[1,128,1024]{2,1,0:T(8,128)(2,1)S(1)}, bf16[1,128,1024]{2,1,0:T(8,128)(2,1)}, u32[]{:S(2)}, u32[]{:S(2)}) collective-permute-start(bf16[1,128,1024]{2,1,0:T(8,128)(2,1)S(1)} %collective-permute-done.2.refs_4_), channel_id=1, source_target_pairs={{0,8},{4,12},{8,0},{12,4},{16,24},{20,28},{24,16},{28,20},{1,9},{5... | collective-permute-start | bytes 786440 | tf_op jit(solution)/shard_map/ppermute | solution.py:29
  23.6 12.3 %collective-permute-start.8 = (bf16[1,128,1024]{2,1,0:T(8,128)(2,1)S(1)}, bf16[1,128,1024]{2,1,0:T(8,128)(2,1)}, u32[]{:S(2)}, u32[]{:S(2)}) collective-permute-start(bf16[1,128,1024]{2,1,0:T(8,128)(2,1)S(1)} %collective-permute-done.2.refs_4_), channel_id=1, source_target_pairs={{0,4},{4,0},{8,12},{12,8},{16,20},{20,16},{24,28},{28,24},{1,5},{5... | collective-permute-start | bytes 786440 | tf_op jit(solution)/shard_map/ppermute | solution.py:29
  35.9 14.7 %collective-permute-start.10 = (bf16[256,1024]{1,0:T(8,128)(2,1)S(1)}, bf16[256,1024]{1,0:T(8,128)(2,1)S(1)}, u32[]{:S(2)}, u32[]{:S(2)}) collective-permute-start(bf16[256,1024]{1,0:T(8,128)(2,1)S(1)} %collective-permute-done.5.refs_1_.pair_ref), channel_id=1, source_target_pairs={{0,1},{1,0},{2,3},{3,2},{4,5},{5,4},{6,7},{7,6},{8,9},{9,8},{10,11... | collective-permute-start | bytes 1572872 | tf_op jit(solution)/shard_map/ppermute | solution.py:29
  35.9 14.6 %collective-permute-start.9 = (bf16[256,1024]{1,0:T(8,128)(2,1)S(1)}, bf16[256,1024]{1,0:T(8,128)(2,1)S(1)}, u32[]{:S(2)}, u32[]{:S(2)}) collective-permute-start(bf16[256,1024]{1,0:T(8,128)(2,1)S(1)} %copy-done.2), channel_id=1, source_target_pairs={{0,1},{1,0},{2,3},{3,2},{4,5},{5,4},{6,7},{7,6},{8,9},{9,8},{10,11... | collective-permute-start | bytes 1572872 | tf_op jit(solution)/shard_map/ppermute | solution.py:29
  36.4 9.4 %collective-permute-start.11 = (bf16[1,128,1024]{2,1,0:T(8,128)(2,1)}, bf16[1,128,1024]{2,1,0:T(8,128)(2,1)S(1)}, u32[]{:S(2)}, u32[]{:S(2)}) collective-permute-start(bf16[1,128,1024]{2,1,0:T(8,128)(2,1)} %collective-permute-done.6.refs_2_), channel_id=1, source_target_pairs={{0,4},{4,0},{8,12},{12,8},{16,20},{20,16},{24,28},{28,24},{1,5},{5... | collective-permute-start | bytes 786440 | tf_op jit(solution)/shard_map/ppermute | solution.py:29
  38.0 12.6 %collective-permute-start.12 = (bf16[1,128,1024]{2,1,0:T(8,128)(2,1)}, bf16[1,128,1024]{2,1,0:T(8,128)(2,1)S(1)}, u32[]{:S(2)}, u32[]{:S(2)}) collective-permute-start(bf16[1,128,1024]{2,1,0:T(8,128)(2,1)} %collective-permute-done.7.refs_6_), channel_id=1, source_target_pairs={{0,4},{4,0},{8,12},{12,8},{16,20},{20,16},{24,28},{28,24},{1,5},{5... | collective-permute-start | bytes 786440 | tf_op jit(solution)/shard_map/ppermute | solution.py:29
  38.5 32.0 %collective-permute-start.13 = (bf16[1,128,1024]{2,1,0:T(8,128)(2,1)S(1)}, bf16[1,128,1024]{2,1,0:T(8,128)(2,1)S(1)}, u32[]{:S(2)}, u32[]{:S(2)}) collective-permute-start(bf16[1,128,1024]{2,1,0:T(8,128)(2,1)S(1)} %bitcast.53), channel_id=1, source_target_pairs={{0,16},{4,20},{8,24},{12,28},{16,0},{20,4},{24,8},{28,12},{1,17},{... | collective-permute-start | bytes 786440 | tf_op jit(solution)/shard_map/ppermute | solution.py:29
  50.6 19.9 %collective-permute-start.14 = (bf16[1,128,1024]{2,1,0:T(8,128)(2,1)S(1)}, bf16[1,128,1024]{2,1,0:T(8,128)(2,1)}, u32[]{:S(2)}, u32[]{:S(2)}) collective-permute-start(bf16[1,128,1024]{2,1,0:T(8,128)(2,1)S(1)} %bitcast.54), channel_id=1, source_target_pairs={{0,8},{4,12},{8,0},{12,4},{16,24},{20,28},{24,16},{28,20},{1,9},{5... | collective-permute-start | bytes 786440 | tf_op jit(solution)/shard_map/ppermute | solution.py:29
  51.5 19.1 %collective-permute-start.15 = (bf16[1,128,1024]{2,1,0:T(8,128)(2,1)S(1)}, bf16[1,128,1024]{2,1,0:T(8,128)(2,1)S(1)}, u32[]{:S(2)}, u32[]{:S(2)}) collective-permute-start(bf16[1,128,1024]{2,1,0:T(8,128)(2,1)S(1)} %bitcast.55), channel_id=1, source_target_pairs={{0,4},{4,0},{8,12},{12,8},{16,20},{20,16},{24,28},{28,24},{1,5},{5... | collective-permute-start | bytes 786440 | tf_op jit(solution)/shard_map/ppermute | solution.py:29
  77.9 25.9 %collective-permute-start.22 = (bf16[512,1024]{1,0:T(8,128)(2,1)}, bf16[512,1024]{1,0:T(8,128)(2,1)S(1)}, u32[]{:S(2)}, u32[]{:S(2)}) collective-permute-start(bf16[512,1024]{1,0:T(8,128)(2,1)} %low_rows.4), channel_id=1, source_target_pairs={{0,2},{1,3},{2,0},{3,1},{4,6},{5,7},{6,4},{7,5},{8,10},{9,11},{10,... | collective-permute-start | bytes 3145736 | tf_op jit(solution)/shard_map/ppermute | solution.py:29
  79.4 13.1 %collective-permute-start.17 = (bf16[1,128,1024]{2,1,0:T(8,128)(2,1)S(1)}, bf16[1,128,1024]{2,1,0:T(8,128)(2,1)S(1)}, u32[]{:S(2)}, u32[]{:S(2)}) collective-permute-start(bf16[1,128,1024]{2,1,0:T(8,128)(2,1)S(1)} %copy-done.30), channel_id=1, source_target_pairs={{0,8},{4,12},{8,0},{12,4},{16,24},{20,28},{24,16},{28,20},{1,9},{5... | collective-permute-start | bytes 786440 | tf_op jit(solution)/shard_map/ppermute | solution.py:29
  80.6 15.4 %collective-permute-start.18 = (bf16[1,128,1024]{2,1,0:T(8,128)(2,1)S(1)}, bf16[1,128,1024]{2,1,0:T(8,128)(2,1)S(1)}, u32[]{:S(2)}, u32[]{:S(2)}) collective-permute-start(bf16[1,128,1024]{2,1,0:T(8,128)(2,1)S(1)} %copy-done.30), channel_id=1, source_target_pairs={{0,4},{4,0},{8,12},{12,8},{16,20},{20,16},{24,28},{28,24},{1,5},{5... | collective-permute-start | bytes 786440 | tf_op jit(solution)/shard_map/ppermute | solution.py:29
  81.2 14.9 %collective-permute-start.19 = (bf16[1,128,1024]{2,1,0:T(8,128)(2,1)}, bf16[1,128,1024]{2,1,0:T(8,128)(2,1)S(1)}, u32[]{:S(2)}, u32[]{:S(2)}) collective-permute-start(bf16[1,128,1024]{2,1,0:T(8,128)(2,1)} %collective-permute-done.14.refs_2_), channel_id=1, source_target_pairs={{0,4},{4,0},{8,12},{12,8},{16,20},{20,16},{24,28},{28,24},{1,5},{5... | collective-permute-start | bytes 786440 | tf_op jit(solution)/shard_map/ppermute | solution.py:29
  82.7 13.8 %collective-permute-start.20 = (bf16[1,1024,128]{2,1,0:T(8,128)(2,1)S(1)}, bf16[1,1024,128]{2,1,0:T(8,128)(2,1)S(1)}, u32[]{:S(2)}, u32[]{:S(2)}) collective-permute-start(bf16[1,1024,128]{2,1,0:T(8,128)(2,1)S(1)} %bitcast.49), channel_id=1, source_target_pairs={{0,16},{4,20},{8,24},{12,28},{16,0},{20,4},{24,8},{28,12},{1,17},{... | collective-permute-start | bytes 786440 | tf_op jit(solution)/shard_map/ppermute | solution.py:29
  99.7 10.3 %collective-permute-start.23 = (bf16[1,1024,128]{2,1,0:T(8,128)(2,1)S(1)}, bf16[1,1024,128]{2,1,0:T(8,128)(2,1)S(1)}, u32[]{:S(2)}, u32[]{:S(2)}) collective-permute-start(bf16[1,1024,128]{2,1,0:T(8,128)(2,1)S(1)} %bitcast.51), channel_id=1, source_target_pairs={{0,8},{4,12},{8,0},{12,4},{16,24},{20,28},{24,16},{28,20},{1,9},{5... | collective-permute-start | bytes 786440 | tf_op jit(solution)/shard_map/ppermute | solution.py:29
  100.5 11.1 %collective-permute-start.24 = (bf16[1,1024,128]{2,1,0:T(8,128)(2,1)S(1)}, bf16[1,1024,128]{2,1,0:T(8,128)(2,1)S(1)}, u32[]{:S(2)}, u32[]{:S(2)}) collective-permute-start(bf16[1,1024,128]{2,1,0:T(8,128)(2,1)S(1)} %collective-permute-done.20.refs_4_), channel_id=1, source_target_pairs={{0,8},{4,12},{8,0},{12,4},{16,24},{20,28},{24,16},{28,20},{1,9},{5... | collective-permute-start | bytes 786440 | tf_op jit(solution)/shard_map/ppermute | solution.py:29
  101.7 9.9 %collective-permute-start.25 = (bf16[1,1024,128]{2,1,0:T(8,128)(2,1)S(1)}, bf16[1,1024,128]{2,1,0:T(8,128)(2,1)S(1)}, u32[]{:S(2)}, u32[]{:S(2)}) collective-permute-start(bf16[1,1024,128]{2,1,0:T(8,128)(2,1)S(1)} %collective-permute-done.20.refs_4_), channel_id=1, source_target_pairs={{0,4},{4,0},{8,12},{12,8},{16,20},{20,16},{24,28},{28,24},{1,5},{5... | collective-permute-start | bytes 786440 | tf_op jit(solution)/shard_map/ppermute | solution.py:29
  102.2 10.8 %collective-permute-start.26 = (bf16[1,128,1024]{2,1,0:T(8,128)(2,1)S(1)}, bf16[1,128,1024]{2,1,0:T(8,128)(2,1)S(1)}, u32[]{:S(2)}, u32[]{:S(2)}) collective-permute-start(bf16[1,128,1024]{2,1,0:T(8,128)(2,1)S(1)} %collective-permute-done.17.refs_6_), channel_id=1, source_target_pairs={{0,4},{4,0},{8,12},{12,8},{16,20},{20,16},{24,28},{28,24},{1,5},{5... | collective-permute-start | bytes 786440 | tf_op jit(solution)/shard_map/ppermute | solution.py:29
  113.1 8.9 %collective-permute-start.27 = (bf16[512,1024]{1,0:T(8,128)(2,1)}, bf16[512,1024]{1,0:T(8,128)(2,1)S(1)}, u32[]{:S(2)}, u32[]{:S(2)}) collective-permute-start(bf16[512,1024]{1,0:T(8,128)(2,1)} %get-tuple-element.339.in_ref.refs_0_), channel_id=1, source_target_pairs={{0,1},{1,0},{2,3},{3,2},{4,5},{5,4},{6,7},{7,6},{8,9},{9,8},{10,11... | collective-permute-start | bytes 3145736 | tf_op jit(solution)/shard_map/ppermute | solution.py:29
  113.1 17.0 %collective-permute-start.28 = (bf16[1,1024,128]{2,1,0:T(8,128)(2,1)S(1)}, bf16[1,1024,128]{2,1,0:T(8,128)(2,1)S(1)}, u32[]{:S(2)}, u32[]{:S(2)}) collective-permute-start(bf16[1,1024,128]{2,1,0:T(8,128)(2,1)S(1)} %collective-permute-done.23.refs_2_), channel_id=1, source_target_pairs={{0,4},{4,0},{8,12},{12,8},{16,20},{20,16},{24,28},{28,24},{1,5},{5... | collective-permute-start | bytes 786440 | tf_op jit(solution)/shard_map/ppermute | solution.py:29
  113.6 16.5 %collective-permute-start.29 = (bf16[1,1024,128]{2,1,0:T(8,128)(2,1)S(1)}, bf16[1,1024,128]{2,1,0:T(8,128)(2,1)S(1)}, u32[]{:S(2)}, u32[]{:S(2)}) collective-permute-start(bf16[1,1024,128]{2,1,0:T(8,128)(2,1)S(1)} %collective-permute-done.24.refs_6_), channel_id=1, source_target_pairs={{0,4},{4,0},{8,12},{12,8},{16,20},{20,16},{24,28},{28,24},{1,5},{5... | collective-permute-start | bytes 786440 | tf_op jit(solution)/shard_map/ppermute | solution.py:29
  169.8 25.6 %collective-permute-start.34 = (bf16[512,1024]{1,0:T(8,128)(2,1)}, bf16[512,1024]{1,0:T(8,128)(2,1)S(1)}, u32[]{:S(2)}, u32[]{:S(2)}) collective-permute-start(bf16[512,1024]{1,0:T(8,128)(2,1)} %low_rows.5), channel_id=1, source_target_pairs={{0,2},{1,3},{2,0},{3,1},{4,6},{5,7},{6,4},{7,5},{8,10},{9,11},{10,... | collective-permute-start | bytes 3145736 | tf_op jit(solution)/shard_map/ppermute | solution.py:29
  170.9 25.1 %collective-permute-start.35 = (bf16[1024,512]{1,0:T(8,128)(2,1)S(1)}, bf16[1024,512]{1,0:T(8,128)(2,1)S(1)}, u32[]{:S(2)}, u32[]{:S(2)}) collective-permute-start(bf16[1024,512]{1,0:T(8,128)(2,1)S(1)} %copy-done.47), channel_id=1, source_target_pairs={{0,8},{4,12},{8,0},{12,4},{16,24},{20,28},{24,16},{28,20},{1,9},{5... | collective-permute-start | bytes 3145736 | tf_op jit(solution)/shard_map/ppermute | solution.py:29
  179.2 31.0 %collective-permute-start.36 = (bf16[512,1024]{1,0:T(8,128)(2,1)}, bf16[512,1024]{1,0:T(8,128)(2,1)}, u32[]{:S(2)}, u32[]{:S(2)}) collective-permute-start(bf16[512,1024]{1,0:T(8,128)(2,1)} %get-tuple-element.407), channel_id=1, source_target_pairs={{0,4},{4,0},{8,12},{12,8},{16,20},{20,16},{24,28},{28,24},{1,5},{5... | collective-permute-start | bytes 3145736 | tf_op jit(solution)/shard_map/ppermute | solution.py:29
  199.9 10.3 %collective-permute-start.37 = (bf16[512,1024]{1,0:T(8,128)(2,1)}, bf16[512,1024]{1,0:T(8,128)(2,1)S(1)}, u32[]{:S(2)}, u32[]{:S(2)}) collective-permute-start(bf16[512,1024]{1,0:T(8,128)(2,1)} %get-tuple-element.408), channel_id=1, source_target_pairs={{0,1},{1,0},{2,3},{3,2},{4,5},{5,4},{6,7},{7,6},{8,9},{9,8},{10,11... | collective-permute-start | bytes 3145736 | tf_op jit(solution)/shard_map/ppermute | solution.py:29
  199.9 62.4 %collective-permute-start.43 = (bf16[1024,256]{1,0:T(8,128)(2,1)}, bf16[1024,256]{1,0:T(8,128)(2,1)S(1)}, u32[]{:S(2)}, u32[]{:S(2)}) collective-permute-start(bf16[1024,256]{1,0:T(8,128)(2,1)} %get-tuple-element.461), channel_id=1, source_target_pairs={{0,16},{4,20},{8,24},{12,28},{16,0},{20,4},{24,8},{28,12},{1,17},{... | collective-permute-start | bytes 1572872 | tf_op jit(solution)/shard_map/ppermute | solution.py:29
  220.7 18.9 %collective-permute-start.39 = (bf16[256,1024]{1,0:T(8,128)(2,1)S(1)}, bf16[256,1024]{1,0:T(8,128)(2,1)S(1)}, u32[]{:S(2)}, u32[]{:S(2)}) collective-permute-start(bf16[256,1024]{1,0:T(8,128)(2,1)S(1)} %copy-done.53), channel_id=1, source_target_pairs={{0,8},{4,12},{8,0},{12,4},{16,24},{20,28},{24,16},{28,20},{1,9},{5... | collective-permute-start | bytes 1572872 | tf_op jit(solution)/shard_map/ppermute | solution.py:29
  222.4 17.2 %collective-permute-start.40 = (bf16[256,1024]{1,0:T(8,128)(2,1)S(1)}, bf16[256,1024]{1,0:T(8,128)(2,1)S(1)}, u32[]{:S(2)}, u32[]{:S(2)}) collective-permute-start(bf16[256,1024]{1,0:T(8,128)(2,1)S(1)} %copy-done.51), channel_id=1, source_target_pairs={{0,2},{1,3},{2,0},{3,1},{4,6},{5,7},{6,4},{7,5},{8,10},{9,11},{10,... | collective-permute-start | bytes 1572872 | tf_op jit(solution)/shard_map/ppermute | solution.py:29
  223.2 16.3 %collective-permute-start.41 = (bf16[256,512]{1,0:T(8,128)(2,1)}, bf16[256,512]{1,0:T(8,128)(2,1)S(1)}, u32[]{:S(2)}, u32[]{:S(2)}) collective-permute-start(bf16[256,512]{1,0:T(8,128)(2,1)} %get-tuple-element.435), channel_id=1, source_target_pairs={{0,4},{4,0},{8,12},{12,8},{16,20},{20,16},{24,28},{28,24},{1,5},{5... | collective-permute-start | bytes 786440 | tf_op jit(solution)/shard_map/ppermute | solution.py:29
  248.4 14.0 %collective-permute-start.42 = (bf16[512,384]{1,0:T(8,128)(2,1)}, bf16[512,384]{1,0:T(8,128)(2,1)S(1)}, u32[]{:S(2)}, u32[]{:S(2)}) collective-permute-start(bf16[512,384]{1,0:T(8,128)(2,1)} %get-tuple-element.460), channel_id=1, source_target_pairs={{0,4},{4,0},{8,12},{12,8},{16,20},{20,16},{24,28},{28,24},{1,5},{5... | collective-permute-start | bytes 1179656 | tf_op jit(solution)/shard_map/ppermute | solution.py:29
  249.9 12.5 %collective-permute-start.44 = (bf16[256,256]{1,0:T(8,128)(2,1)S(1)}, bf16[256,256]{1,0:T(8,128)(2,1)S(1)}, u32[]{:S(2)}, u32[]{:S(2)}) collective-permute-start(bf16[256,256]{1,0:T(8,128)(2,1)S(1)} %copy-done.61), channel_id=1, source_target_pairs={{0,8},{4,12},{8,0},{12,4},{16,24},{20,28},{24,16},{28,20},{1,9},{5... | collective-permute-start | bytes 393224 | tf_op jit(solution)/shard_map/ppermute | solution.py:29
  254.4 16.1 %collective-permute-start.47 = (bf16[128,1024]{1,0:T(8,128)(2,1)}, bf16[128,1024]{1,0:T(8,128)(2,1)S(1)}, u32[]{:S(2)}, u32[]{:S(2)}) collective-permute-start(bf16[128,1024]{1,0:T(8,128)(2,1)} %get-tuple-element.477), channel_id=1, source_target_pairs={{0,16},{4,20},{8,24},{12,28},{16,0},{20,4},{24,8},{28,12},{1,17},{... | collective-permute-start | bytes 786440 | tf_op jit(solution)/shard_map/ppermute | solution.py:29
  262.4 8.1 %collective-permute-start.46 = (f32[24,1024]{1,0:T(8,128)}, f32[24,1024]{1,0:T(8,128)S(1)}, u32[]{:S(2)}, u32[]{:S(2)}) collective-permute-start(f32[24,1024]{1,0:T(8,128)} %get-tuple-element.472), channel_id=1, source_target_pairs={{0,1},{1,0},{2,3},{3,2},{4,5},{5,4},{6,7},{7,6},{8,9},{9,8},{10,11... | collective-permute-start | bytes 294920 | tf_op jit(solution)/shard_map/ppermute | solution.py:29
  262.5 8.0 %collective-permute-start.45 = (bf16[512,1024]{1,0:T(8,128)(2,1)}, bf16[512,1024]{1,0:T(8,128)(2,1)S(1)}, u32[]{:S(2)}, u32[]{:S(2)}) collective-permute-start(bf16[512,1024]{1,0:T(8,128)(2,1)} %get-tuple-element.470), channel_id=1, source_target_pairs={{0,1},{1,0},{2,3},{3,2},{4,5},{5,4},{6,7},{7,6},{8,9},{9,8},{10,11... | collective-permute-start | bytes 3145736 | tf_op jit(solution)/shard_map/ppermute | solution.py:29
  263.0 16.3 %collective-permute-start.50 = (bf16[512,384]{1,0:T(8,128)(2,1)S(1)}, bf16[512,384]{1,0:T(8,128)(2,1)S(1)}, u32[]{:S(2)}, u32[]{:S(2)}) collective-permute-start(bf16[512,384]{1,0:T(8,128)(2,1)S(1)} %copy-done.54), channel_id=1, source_target_pairs={{0,4},{4,0},{8,12},{12,8},{16,20},{20,16},{24,28},{28,24},{1,5},{5... | collective-permute-start | bytes 1179656 | tf_op jit(solution)/shard_map/ppermute | solution.py:29
  270.5 8.8 %collective-permute-start.48 = (f32[24,1024]{1,0:T(8,128)S(1)}, f32[24,1024]{1,0:T(8,128)S(1)}, u32[]{:S(2)}, u32[]{:S(2)}) collective-permute-start(f32[24,1024]{1,0:T(8,128)S(1)} %add.84), channel_id=1, source_target_pairs={{0,2},{1,3},{2,0},{3,1},{4,6},{5,7},{6,4},{7,5},{8,10},{9,11},{10,... | collective-permute-start | bytes 294920 | tf_op jit(solution)/shard_map/ppermute | solution.py:29
  271.4 7.9 %collective-permute-start.49 = (bf16[256,384]{1,0:T(8,128)(2,1)}, bf16[256,384]{1,0:T(8,128)(2,1)S(1)}, u32[]{:S(2)}, u32[]{:S(2)}) collective-permute-start(bf16[256,384]{1,0:T(8,128)(2,1)} %get-tuple-element.483), channel_id=1, source_target_pairs={{0,8},{4,12},{8,0},{12,4},{16,24},{20,28},{24,16},{28,20},{1,9},{5... | collective-permute-start | bytes 589832 | tf_op jit(solution)/shard_map/ppermute | solution.py:29
  271.4 7.9 %collective-permute-start.51 = (bf16[256,128]{1,0:T(8,128)(2,1)S(1)}, bf16[256,128]{1,0:T(8,128)(2,1)S(1)}, u32[]{:S(2)}, u32[]{:S(2)}) collective-permute-start(bf16[256,128]{1,0:T(8,128)(2,1)S(1)} %copy-done.62), channel_id=1, source_target_pairs={{0,16},{4,20},{8,24},{12,28},{16,0},{20,4},{24,8},{28,12},{1,17},{... | collective-permute-start | bytes 196616 | tf_op jit(solution)/shard_map/ppermute | solution.py:29
  285.7 14.2 %collective-permute-start.55 = (bf16[256,1024]{1,0:T(8,128)(2,1)S(1)}, bf16[256,1024]{1,0:T(8,128)(2,1)S(1)}, u32[]{:S(2)}, u32[]{:S(2)}) collective-permute-start(bf16[256,1024]{1,0:T(8,128)(2,1)S(1)} %copy-done.50), channel_id=1, source_target_pairs={{0,2},{1,3},{2,0},{3,1},{4,6},{5,7},{6,4},{7,5},{8,10},{9,11},{10,... | collective-permute-start | bytes 1572872 | tf_op jit(solution)/shard_map/ppermute | solution.py:29
  286.6 14.6 %collective-permute-start.59 = (bf16[1024,128]{1,0:T(8,128)(2,1)S(1)}, bf16[1024,128]{1,0:T(8,128)(2,1)S(1)}, u32[]{:S(2)}, u32[]{:S(2)}) collective-permute-start(bf16[1024,128]{1,0:T(8,128)(2,1)S(1)} %copy-done.57), channel_id=1, source_target_pairs={{0,4},{4,0},{8,12},{12,8},{16,20},{20,16},{24,28},{28,24},{1,5},{5... | collective-permute-start | bytes 786440 | tf_op jit(solution)/shard_map/ppermute | solution.py:29
  299.9 9.0 %collective-permute-start.58 = (bf16[128,384]{1,0:T(8,128)(2,1)}, bf16[128,384]{1,0:T(8,128)(2,1)S(1)}, u32[]{:S(2)}, u32[]{:S(2)}) collective-permute-start(bf16[128,384]{1,0:T(8,128)(2,1)} %get-tuple-element.515), channel_id=1, source_target_pairs={{0,16},{4,20},{8,24},{12,28},{16,0},{20,4},{24,8},{28,12},{1,17},{... | collective-permute-start | bytes 294920 | tf_op jit(solution)/shard_map/ppermute | solution.py:29
  302.0 8.0 %collective-permute-start.56 = (f32[24,1024]{1,0:T(8,128)S(1)}, f32[24,1024]{1,0:T(8,128)S(1)}, u32[]{:S(2)}, u32[]{:S(2)}) collective-permute-start(f32[24,1024]{1,0:T(8,128)S(1)} %add.87), channel_id=1, source_target_pairs={{0,16},{4,20},{8,24},{12,28},{16,0},{20,4},{24,8},{28,12},{1,17},{... | collective-permute-start | bytes 294920 | tf_op jit(solution)/shard_map/ppermute | solution.py:29
  (76 other events, 595.1 us)
